TPU v7x, 32 devices: a whole 2x2x4 slice. The times are simulated.
32 devices in a mesh: fsdp: 16 (over z, x, core), seq: 2 (over y).
Axes of the slice: x: 2, y: 2, z: 4, core: 2. Of those that a mesh axis runs over, the one named last changes fastest.
Arguments:
- clips: bfloat16 [32, 1024, 1024], P('fsdp', 'seq'), may hold values from -6 to 6
- cotangent: bfloat16 [32, 1024, 1024], P('fsdp', 'seq'), may hold values from -6 to 6
- valid: int32 [32], P('fsdp'), may hold values 0 or 1
- norm1_gain: bfloat16 [1024], P('fsdp'), may hold values from 0.5 to 1.5
- norm1_bias: bfloat16 [1024], P('fsdp'), may hold values from -1.5 to 1.5
- query_weight: bfloat16 [1024, 1024], P('fsdp'), may hold values from -0.1875 to 0.1875
- key_weight: bfloat16 [1024, 1024], P('fsdp'), may hold values from -0.1875 to 0.1875
- value_weight: bfloat16 [1024, 1024], P('fsdp'), may hold values from -0.1875 to 0.1875
- query_bias: bfloat16 [1024], P('fsdp'), may hold values from -1.5 to 1.5
- value_bias: bfloat16 [1024], P('fsdp'), may hold values from -1.5 to 1.5
- proj_weight: bfloat16 [1024, 1024], P('fsdp'), may hold values from -2 to 2
- proj_bias: bfloat16 [1024], P('fsdp'), may hold values from -1.5 to 1.5
- norm2_gain: bfloat16 [1024], P('fsdp'), may hold values from 0.5 to 1.5
- norm2_bias: bfloat16 [1024], P('fsdp'), may hold values from -1.5 to 1.5
- fc1_weight: bfloat16 [1024, 4096], P('fsdp'), may hold values from -0.1875 to 0.1875
- fc1_bias: bfloat16 [4096], P('fsdp'), may hold values from -1.5 to 1.5
- fc2_weight: bfloat16 [4096, 1024], P('fsdp'), may hold values from -0.09375 to 0.09375
- fc2_bias: bfloat16 [1024], P('fsdp'), may hold values from -1.5 to 1.5
Outputs:
- layer_out: bfloat16 [32, 1024, 1024], P('fsdp', 'seq')
- grad_clips: float32 [32, 1024, 1024], P('fsdp', 'seq')
- grad_norm1_gain: float32 [1024], P('fsdp')
- grad_norm1_bias: float32 [1024], P('fsdp')
- grad_query_weight: float32 [1024, 1024], P('fsdp')
- grad_key_weight: float32 [1024, 1024], P('fsdp')
- grad_value_weight: float32 [1024, 1024], P('fsdp')
- grad_query_bias: float32 [1024], P('fsdp')
- grad_value_bias: float32 [1024], P('fsdp')
- grad_proj_weight: float32 [1024, 1024], P('fsdp')
- grad_proj_bias: float32 [1024], P('fsdp')
- grad_norm2_gain: float32 [1024], P('fsdp')
- grad_norm2_bias: float32 [1024], P('fsdp')
- grad_fc1_weight: float32 [1024, 4096], P('fsdp')
- grad_fc1_bias: float32 [4096], P('fsdp')
- grad_fc2_weight: float32 [4096, 1024], P('fsdp')
- grad_fc2_bias: float32 [1024], P('fsdp')
Inputs may be any that keep to these rules, and one draw needn't show every extreme that they name: Padding clips (valid 0) contribute nothing to any gradient.
All inputs are finite; a program needn't handle non-finite values. No bound on the sum of `valid` on one device may be relied on, other than what follows from the above.
Results may differ from a plain program's by a relative error of at most 0.023.
Values may be sent and summed in bfloat16 or wider, within the bound.
A program may use at most 256 MiB of HBM per device.

v0:
```python
import jax
import jax.numpy as jnp
from jax import lax
from jax.sharding import PartitionSpec as P

H = 16
QBLK = 512


norm_eps = 1e-06
root_half = 0.7071067811865476
inv_root_tau = 0.3989422804014327


def matmul(left, right):
    return jnp.dot(left, right, preferred_element_type=jnp.float32)


def matmul_nt(left, right):
    return lax.dot_general(
        left, right, (((1,), (1,)), ((), ())), preferred_element_type=jnp.float32
    )


def matmul_tn(left, right):
    return lax.dot_general(
        left, right, (((0,), (0,)), ((), ())), preferred_element_type=jnp.float32
    )


def layer_norm(values_in, gain, shift):
    row_mean = jnp.mean(values_in, axis=-1, keepdims=True)
    centred = values_in - row_mean
    inverse = lax.rsqrt(jnp.mean(centred * centred, axis=-1, keepdims=True) + norm_eps)
    scaled = centred * inverse
    return (scaled * gain + shift, scaled, inverse)


def layer_norm_back(upstream, scaled, inverse, gain):
    dscaled = upstream * gain
    inner = (
        dscaled
        - jnp.mean(dscaled, axis=-1, keepdims=True)
        - scaled * jnp.mean(dscaled * scaled, axis=-1, keepdims=True)
    )
    return (inverse * inner, jnp.sum(upstream * scaled, axis=0), jnp.sum(upstream, axis=0))


def gelu_value(pre_act):
    return 0.5 * pre_act * (1.0 + lax.erf(pre_act * root_half))


def gelu_slope(pre_act):
    return 0.5 * (1.0 + lax.erf(pre_act * root_half)) + pre_act * inv_root_tau * jnp.exp(
        -0.5 * pre_act * pre_act
    )


def attend(queries, keys_all, values_all, head_count):
    length = queries.shape[0]
    head_width = queries.shape[1] // head_count
    score_scale = head_width ** (-0.5)
    query_heads = queries.reshape(length // QBLK, QBLK, head_count, head_width)
    key_heads = keys_all.reshape(length, head_count, head_width)
    value_heads = values_all.reshape(length, head_count, head_width)

    def one_block(query_rows):
        scores = (
            jnp.einsum("qhd,khd->hqk", query_rows, key_heads, preferred_element_type=jnp.float32)
            * score_scale
        )
        peak = jnp.max(scores, axis=-1, keepdims=True)
        raised = jnp.exp(scores - peak)
        row_total = jnp.sum(raised, axis=-1, keepdims=True)
        weights = (raised / row_total).astype(jnp.bfloat16)
        mixed = jnp.einsum("hqk,khd->qhd", weights, value_heads, preferred_element_type=jnp.float32)
        return (mixed.astype(jnp.bfloat16), (peak + jnp.log(row_total))[:, :, 0])

    mixed, log_totals = lax.map(one_block, query_heads)
    return (mixed.reshape(length, head_count * head_width), log_totals)


def attend_back(queries, keys_all, values_all, log_totals, upstream, head_count):
    length = queries.shape[0]
    head_width = queries.shape[1] // head_count
    score_scale = head_width ** (-0.5)
    query_heads = queries.reshape(length // QBLK, QBLK, head_count, head_width)
    upstream_heads = upstream.reshape(length // QBLK, QBLK, head_count, head_width)
    key_heads = keys_all.reshape(length, head_count, head_width)
    value_heads = values_all.reshape(length, head_count, head_width)

    def one_block(running, block_item):
        key_grad, value_grad = running
        query_rows, log_rows, grad_rows = block_item
        scores = (
            jnp.einsum("qhd,khd->hqk", query_rows, key_heads, preferred_element_type=jnp.float32)
            * score_scale
        )
        weights = jnp.exp(scores - log_rows[:, :, None])
        weights_low = weights.astype(jnp.bfloat16)
        grad_weights = jnp.einsum(
            "qhd,khd->hqk", grad_rows, value_heads, preferred_element_type=jnp.float32
        )
        inner = jnp.sum(grad_weights * weights, axis=-1, keepdims=True)
        grad_scores = (weights * (grad_weights - inner)).astype(jnp.bfloat16)
        query_grad = (
            jnp.einsum("hqk,khd->qhd", grad_scores, key_heads, preferred_element_type=jnp.float32)
            * score_scale
        )
        key_grad = (
            key_grad
            + jnp.einsum(
                "hqk,qhd->khd", grad_scores, query_rows, preferred_element_type=jnp.float32
            )
            * score_scale
        )
        value_grad = value_grad + jnp.einsum(
            "hqk,qhd->khd", weights_low, grad_rows, preferred_element_type=jnp.float32
        )
        return ((key_grad, value_grad), query_grad.astype(jnp.bfloat16))

    zeros_heads = jnp.zeros((length, head_count, head_width), jnp.float32)
    (key_grad, value_grad), query_grad = lax.scan(
        one_block, (zeros_heads, zeros_heads), (query_heads, log_totals, upstream_heads)
    )
    width_all = head_count * head_width
    return (
        query_grad.reshape(length, width_all),
        key_grad.reshape(length, width_all).astype(jnp.bfloat16),
        value_grad.reshape(length, width_all).astype(jnp.bfloat16),
    )


def fetch(shards):
    return (
        lax.all_gather(shards[0], "fsdp", axis=0, tiled=True),
        lax.all_gather(shards[1], "fsdp", axis=0, tiled=True),
        lax.all_gather(shards[2], "fsdp", axis=0, tiled=True),
        lax.all_gather(shards[3], "fsdp", axis=0, tiled=True),
        lax.all_gather(shards[4], "fsdp", axis=0, tiled=True),
        lax.all_gather(shards[5], "fsdp", axis=0, tiled=True),
        lax.all_gather(shards[6], "fsdp", axis=0, tiled=True),
        lax.all_gather(shards[7], "fsdp", axis=0, tiled=True),
        lax.all_gather(shards[8], "fsdp", axis=0, tiled=True),
        lax.all_gather(shards[9], "fsdp", axis=0, tiled=True),
        lax.all_gather(shards[10], "fsdp", axis=0, tiled=True),
        lax.all_gather(shards[11], "fsdp", axis=0, tiled=True),
        lax.all_gather(shards[12], "fsdp", axis=0, tiled=True),
        lax.all_gather(shards[13], "fsdp", axis=0, tiled=True),
        lax.all_gather(shards[14], "fsdp", axis=0, tiled=True),
    )


def settle(grads):
    shares = (
        lax.psum_scatter(
            grads[0].astype(jnp.bfloat16), "fsdp", scatter_dimension=0, tiled=True
        ).astype(jnp.float32),
        lax.psum_scatter(
            grads[1].astype(jnp.bfloat16), "fsdp", scatter_dimension=0, tiled=True
        ).astype(jnp.float32),
        lax.psum_scatter(
            grads[2].astype(jnp.bfloat16), "fsdp", scatter_dimension=0, tiled=True
        ).astype(jnp.float32),
        lax.psum_scatter(
            grads[3].astype(jnp.bfloat16), "fsdp", scatter_dimension=0, tiled=True
        ).astype(jnp.float32),
        lax.psum_scatter(
            grads[4].astype(jnp.bfloat16), "fsdp", scatter_dimension=0, tiled=True
        ).astype(jnp.float32),
        lax.psum_scatter(
            grads[5].astype(jnp.bfloat16), "fsdp", scatter_dimension=0, tiled=True
        ).astype(jnp.float32),
        lax.psum_scatter(
            grads[6].astype(jnp.bfloat16), "fsdp", scatter_dimension=0, tiled=True
        ).astype(jnp.float32),
        lax.psum_scatter(
            grads[7].astype(jnp.bfloat16), "fsdp", scatter_dimension=0, tiled=True
        ).astype(jnp.float32),
        lax.psum_scatter(
            grads[8].astype(jnp.bfloat16), "fsdp", scatter_dimension=0, tiled=True
        ).astype(jnp.float32),
        lax.psum_scatter(
            grads[9].astype(jnp.bfloat16), "fsdp", scatter_dimension=0, tiled=True
        ).astype(jnp.float32),
        lax.psum_scatter(
            grads[10].astype(jnp.bfloat16), "fsdp", scatter_dimension=0, tiled=True
        ).astype(jnp.float32),
        lax.psum_scatter(
            grads[11].astype(jnp.bfloat16), "fsdp", scatter_dimension=0, tiled=True
        ).astype(jnp.float32),
        lax.psum_scatter(
            grads[12].astype(jnp.bfloat16), "fsdp", scatter_dimension=0, tiled=True
        ).astype(jnp.float32),
        lax.psum_scatter(
            grads[13].astype(jnp.bfloat16), "fsdp", scatter_dimension=0, tiled=True
        ).astype(jnp.float32),
        lax.psum_scatter(
            grads[14].astype(jnp.bfloat16), "fsdp", scatter_dimension=0, tiled=True
        ).astype(jnp.float32),
    )
    return (
        lax.psum(shares[0].astype(jnp.bfloat16), "seq").astype(jnp.float32),
        lax.psum(shares[1].astype(jnp.bfloat16), "seq").astype(jnp.float32),
        lax.psum(shares[2].astype(jnp.bfloat16), "seq").astype(jnp.float32),
        lax.psum(shares[3].astype(jnp.bfloat16), "seq").astype(jnp.float32),
        lax.psum(shares[4].astype(jnp.bfloat16), "seq").astype(jnp.float32),
        lax.psum(shares[5].astype(jnp.bfloat16), "seq").astype(jnp.float32),
        lax.psum(shares[6].astype(jnp.bfloat16), "seq").astype(jnp.float32),
        lax.psum(shares[7].astype(jnp.bfloat16), "seq").astype(jnp.float32),
        lax.psum(shares[8].astype(jnp.bfloat16), "seq").astype(jnp.float32),
        lax.psum(shares[9].astype(jnp.bfloat16), "seq").astype(jnp.float32),
        lax.psum(shares[10].astype(jnp.bfloat16), "seq").astype(jnp.float32),
        lax.psum(shares[11].astype(jnp.bfloat16), "seq").astype(jnp.float32),
        lax.psum(shares[12].astype(jnp.bfloat16), "seq").astype(jnp.float32),
        lax.psum(shares[13].astype(jnp.bfloat16), "seq").astype(jnp.float32),
        lax.psum(shares[14].astype(jnp.bfloat16), "seq").astype(jnp.float32),
    )


def one_clip(clip_in, clip_cot, clip_flag, gathered, head_count):
    (
        norm1_gain,
        norm1_bias,
        query_weight,
        key_weight,
        value_weight,
        query_bias,
        value_bias,
        proj_weight,
        proj_bias,
        norm2_gain,
        norm2_bias,
        fc1_weight,
        fc1_bias,
        fc2_weight,
        fc2_bias,
    ) = gathered
    gain_one = norm1_gain.astype(jnp.float32)
    gain_two = norm2_gain.astype(jnp.float32)
    tokens_in = clip_in.astype(jnp.float32)
    normed, scaled_one, inverse_one = layer_norm(
        tokens_in, gain_one, norm1_bias.astype(jnp.float32)
    )
    normed_low = normed.astype(jnp.bfloat16)
    queries = (matmul(normed_low, query_weight) + query_bias.astype(jnp.float32)).astype(
        jnp.bfloat16
    )
    keys_all = matmul(normed_low, key_weight).astype(jnp.bfloat16)
    values_all = (matmul(normed_low, value_weight) + value_bias.astype(jnp.float32)).astype(
        jnp.bfloat16
    )
    query_heads, key_heads, value_heads = (
        lax.all_to_all(queries, "seq", split_axis=1, concat_axis=0, tiled=True),
        lax.all_to_all(keys_all, "seq", split_axis=1, concat_axis=0, tiled=True),
        lax.all_to_all(values_all, "seq", split_axis=1, concat_axis=0, tiled=True),
    )
    mixed_heads, log_totals = attend(query_heads, key_heads, value_heads, head_count)
    attended = lax.all_to_all(mixed_heads, "seq", split_axis=0, concat_axis=1, tiled=True)
    middle = tokens_in + matmul(attended, proj_weight) + proj_bias.astype(jnp.float32)
    normed_two, scaled_two, inverse_two = layer_norm(
        middle, gain_two, norm2_bias.astype(jnp.float32)
    )
    normed_two_low = normed_two.astype(jnp.bfloat16)
    hidden_pre = matmul(normed_two_low, fc1_weight) + fc1_bias.astype(jnp.float32)
    hidden_low = gelu_value(hidden_pre).astype(jnp.bfloat16)
    output = middle + matmul(hidden_low, fc2_weight) + fc2_bias.astype(jnp.float32)
    grad_out = clip_cot.astype(jnp.float32) * clip_flag.astype(jnp.float32)
    grad_mlp = grad_out.astype(jnp.bfloat16)
    grad_fc2_weight = matmul_tn(hidden_low, grad_mlp)
    grad_fc2_bias = jnp.sum(grad_mlp.astype(jnp.float32), axis=0)
    grad_pre = (matmul_nt(grad_mlp, fc2_weight) * gelu_slope(hidden_pre)).astype(jnp.bfloat16)
    grad_fc1_weight = matmul_tn(normed_two_low, grad_pre)
    grad_fc1_bias = jnp.sum(grad_pre.astype(jnp.float32), axis=0)
    grad_norm_two = matmul_nt(grad_pre, fc1_weight)
    grad_ln_two, grad_norm2_gain, grad_norm2_bias = layer_norm_back(
        grad_norm_two, scaled_two, inverse_two, gain_two
    )
    grad_middle = grad_out + grad_ln_two
    grad_branch = grad_middle.astype(jnp.bfloat16)
    grad_proj_weight = matmul_tn(attended, grad_branch)
    grad_proj_bias = jnp.sum(grad_branch.astype(jnp.float32), axis=0)
    grad_att = matmul_nt(grad_branch, proj_weight).astype(jnp.bfloat16)
    grad_att_heads = lax.all_to_all(grad_att, "seq", split_axis=1, concat_axis=0, tiled=True)
    query_grad, key_grad, value_grad = attend_back(
        query_heads, key_heads, value_heads, log_totals, grad_att_heads, head_count
    )
    grad_queries, grad_keys, grad_values = (
        lax.all_to_all(query_grad, "seq", split_axis=0, concat_axis=1, tiled=True),
        lax.all_to_all(key_grad, "seq", split_axis=0, concat_axis=1, tiled=True),
        lax.all_to_all(value_grad, "seq", split_axis=0, concat_axis=1, tiled=True),
    )
    grad_query_weight = matmul_tn(normed_low, grad_queries)
    grad_key_weight = matmul_tn(normed_low, grad_keys)
    grad_value_weight = matmul_tn(normed_low, grad_values)
    grad_query_bias = jnp.sum(grad_queries.astype(jnp.float32), axis=0)
    grad_value_bias = jnp.sum(grad_values.astype(jnp.float32), axis=0)
    grad_norm_one = (
        matmul_nt(grad_queries, query_weight)
        + matmul_nt(grad_keys, key_weight)
        + matmul_nt(grad_values, value_weight)
    )
    grad_ln_one, grad_norm1_gain, grad_norm1_bias = layer_norm_back(
        grad_norm_one, scaled_one, inverse_one, gain_one
    )
    grad_in = grad_middle + grad_ln_one
    grads = (
        grad_norm1_gain,
        grad_norm1_bias,
        grad_query_weight,
        grad_key_weight,
        grad_value_weight,
        grad_query_bias,
        grad_value_bias,
        grad_proj_weight,
        grad_proj_bias,
        grad_norm2_gain,
        grad_norm2_bias,
        grad_fc1_weight,
        grad_fc1_bias,
        grad_fc2_weight,
        grad_fc2_bias,
    )
    return (output.astype(jnp.bfloat16), grad_in, grads)


def body(
    clips,
    cotangent,
    valid,
    norm1_gain,
    norm1_bias,
    query_weight,
    key_weight,
    value_weight,
    query_bias,
    value_bias,
    proj_weight,
    proj_bias,
    norm2_gain,
    norm2_bias,
    fc1_weight,
    fc1_bias,
    fc2_weight,
    fc2_bias,
):
    shards = (
        norm1_gain,
        norm1_bias,
        query_weight,
        key_weight,
        value_weight,
        query_bias,
        value_bias,
        proj_weight,
        proj_bias,
        norm2_gain,
        norm2_bias,
        fc1_weight,
        fc1_bias,
        fc2_weight,
        fc2_bias,
    )
    slot_count = clips.shape[0]
    head_count = H // lax.axis_size("seq")
    summed = None
    outputs = []
    grad_list = []
    for batch_slot in range(slot_count):
        gathered = fetch(shards)
        output, grad_in, grads = one_clip(
            clips[batch_slot], cotangent[batch_slot], valid[batch_slot], gathered, head_count
        )
        summed = (
            grads
            if summed is None
            else tuple((older + newer for older, newer in zip(summed, grads)))
        )
        outputs.append(output)
        grad_list.append(grad_in)
    summed = settle(summed)
    return (
        jnp.stack(outputs),
        jnp.stack(grad_list),
        summed[0],
        summed[1],
        summed[2],
        summed[3],
        summed[4],
        summed[5],
        summed[6],
        summed[7],
        summed[8],
        summed[9],
        summed[10],
        summed[11],
        summed[12],
        summed[13],
        summed[14],
    )


def solution(mesh):
    in_specs = (
        P("fsdp", "seq", None),
        P("fsdp", "seq", None),
        P("fsdp"),
        P("fsdp"),
        P("fsdp"),
        P("fsdp", None),
        P("fsdp", None),
        P("fsdp", None),
        P("fsdp"),
        P("fsdp"),
        P("fsdp", None),
        P("fsdp"),
        P("fsdp"),
        P("fsdp"),
        P("fsdp", None),
        P("fsdp"),
        P("fsdp", None),
        P("fsdp"),
    )
    out_specs = (
        P("fsdp", "seq", None),
        P("fsdp", "seq", None),
        P("fsdp"),
        P("fsdp"),
        P("fsdp", None),
        P("fsdp", None),
        P("fsdp", None),
        P("fsdp"),
        P("fsdp"),
        P("fsdp", None),
        P("fsdp"),
        P("fsdp"),
        P("fsdp"),
        P("fsdp", None),
        P("fsdp"),
        P("fsdp", None),
        P("fsdp"),
    )
    return jax.shard_map(body, mesh=mesh, in_specs=in_specs, out_specs=out_specs, check_vma=False)
```

profile of v0, /device:TPU:0, one launch (start us, length us, event | category | flops | bytes accessed | tf_op | source)
XLA Modules:
  0.0 1095.7 jit_solution(4099159091317723000)
XLA Ops:
  18.4 63.4 %all-reduce.18 = (bf16[1024]{0:T(1024)(128)(2,1)S(1)}, bf16[1024]{0:T(1024)(128)(2,1)S(1)}, bf16[1024]{0:T(1024)(128)(2,1)S(1)}, bf16[1024]{0:T(1024)(128)(2,1)S...) all-reduce(bf16[1024]{0:T(1024)(128)(2,1)S(1)} %dynamic-update-slic, ...), channel_id=1, replica_groups=mesh['fsdp'=16,'seq'=2] {'fsdp'}, use_global_device_ids=true, to_apply=%add.2 | all-reduce | flops 7168 | bytes 28672
  106.2 33.3 %all-gather.10.cloned.1.call-done = bf16[1024,1024]{1,0:T(8,128)(2,1)} async-done(((bf16[64,1024]{1,0:T(8,128)(2,1)}), bf16[1024,1024]{1,0:T(8,128)(2,1)}) %all-gather.10.cloned.1.call-update) | async-done | bytes 2097168 | tf_op jit(solution)/shard_map/all_gather | solution.py:139
  168.3 19.2 %all-gather = bf16[16,1,256]{2,1,0:T(2,128)(2,1)S(1)} all-gather(bf16[1,1,256]{2,1,0:T(2,128)(2,1)S(1)} %reshape.481), channel_id=1, replica_groups=mesh['fsdp'=16,'seq'=2] {'fsdp'}, dimensions={0}, use_global_device_ids=true | all-gather | bytes 8704 | tf_op jit(solution)/shard_map/all_gather | solution.py:148
  218.1 21.9 %while.54 = (s32[]{:T(128)}, bf16[2,512,8,64]{1,3,2,0:T(8,128)(2,1)}, f32[2,8,512]{2,1,0:T(8,128)S(1)}, bf16[2,512,8,64]{1,3,2,0:T(8,128)(2,1)S(1)}, bf16[1024,8...) while((s32[]{:T(128)}, bf16[2,512,8,64]{1,3,2,0:T(8,128)(2,1)}, ...), condition=%wide.region_5.6_spmd, body=%wide.region_2.5_spmd.sunk | while | flops 1111748608 | bytes 53609044 | solution.py:79
  257.4 21.9 %while.55 = (s32[]{:T(128)}, bf16[2,512,8,64]{1,3,2,0:T(8,128)(2,1)}, f32[2,8,512]{2,1,0:T(8,128)S(1)}, bf16[2,512,8,64]{1,3,2,0:T(8,128)(2,1)S(1)}, bf16[1024,8...) while((s32[]{:T(128)}, bf16[2,512,8,64]{1,3,2,0:T(8,128)(2,1)}, ...), condition=%wide.region_13.14_spmd, body=%wide.region_10.13_spmd.sunk | while | flops 1111748608 | bytes 53609044 | solution.py:79
  315.0 10.9 multiply_convert_fusion.3
  331.7 13.2 %convert_reduce_fusion = (f32[4096]{0:T(1024)}, bf16[512,4096]{1,0:T(8,128)(2,1)}) fusion(f32[512,4096]{1,0:T(8,128)} %copy-done.94, f32[4096]{0:T(1024)S(1)} %bitcast.464, bf16[4096,1024]{1,0:T(8,128)(2,1)} %all-gather.18.cloned.1.call-done, f32[]{:T(128)} %bitcast.41, bf16[2,512,1024]{2,1,0:T(8,128)(2,1)} %param.27), kind=kOutput, calls=%fused_computation.100 | convolution fusion | flops 4323799040 | bytes 22053376 | tf_op jit(solution)/shard_map/dot_general | solution.py:20
  411.7 88.2 %while.56 = (s32[]{:T(128)}, f32[1024,8,64]{0,2,1:T(8,128)}, f32[1024,8,64]{0,2,1:T(8,128)}, bf16[2,512,8,64]{1,3,2,0:T(8,128)(2,1)}, bf16[2,512,8,64]{1,3,2,0:T...) while((s32[]{:T(128)}, f32[1024,8,64]{0,2,1:T(8,128)}, ...), condition=%wide.region_20.21_spmd.clone, body=%wide.region_18.20_spmd.clone.sunk | while | flops 2737827840 | bytes 274319040 | solution.py:123
  414.1 10.8 multiply_reduce_fusion.20
  425.6 10.5 multiply_convert_fusion.6
  458.0 10.8 multiply_reduce_fusion.20
  469.1 10.4 multiply_convert_fusion.6
  511.8 87.8 %while.57 = (s32[]{:T(128)}, f32[1024,8,64]{0,2,1:T(8,128)}, f32[1024,8,64]{0,2,1:T(8,128)}, bf16[2,512,8,64]{1,3,2,0:T(8,128)(2,1)}, bf16[2,512,8,64]{1,3,2,0:T...) while((s32[]{:T(128)}, f32[1024,8,64]{0,2,1:T(8,128)}, ...), condition=%wide.region_27.28_spmd.clone, body=%wide.region_25.27_spmd.clone.sunk | while | flops 2737827840 | bytes 274319040 | solution.py:123
  514.2 10.8 multiply_reduce_fusion.21
  557.6 10.8 multiply_reduce_fusion.21
  672.1 15.3 %all_to_all.268 = bf16[2,512,512]{1,2,0:T(8,128)(2,1)} all-to-all(bf16[2,512,512]{1,2,0:T(8,128)(2,1)} %bitcast.453), channel_id=1, replica_groups=mesh['fsdp'=16,'seq'=2] {'seq'}, dimensions={0} | all-to-all | bytes 2097152 | tf_op jit(solution)/shard_map/all_to_all | solution.py:289
  708.2 13.3 %fusion.136 = f32[1024,4096]{1,0:T(8,128)} fusion(bf16[512,4096]{1,0:T(8,128)(2,1)} %copy-done.92, f32[512,1024]{1,0:T(8,128)} %copy-done.22, f32[1024]{0:T(1024)S(1)} %copy-done.80, f32[1024]{0:T(1024)S(1)} %copy-done.61, f32[512]{0:T(512)S(1)} %copy-done.76, f32[512]{0:T(512)S(1)} %copy-done.51), kind=kOutput, calls=%fused_computation.247 | convolution fusion | flops 4297588736 | bytes 23080960 | tf_op jit(solution)/shard_map/dot_general | solution.py:26
  721.5 15.8 %add_convert_fusion.1 = bf16[1024,4096]{1,0:T(8,128)(2,1)} fusion(f32[1024,4096]{1,0:T(8,128)} %fusion.136, bf16[512,4096]{1,0:T(8,128)(2,1)} %get-tuple-element.437, f32[512,1024]{1,0:T(8,128)} %copy-done.26, f32[512]{0:T(512)S(1)} %copy-done.74, f32[512]{0:T(512)S(1)} %copy-done.53, f32[1024]{0:T(1024)S(1)} %copy-done.80, f32[1024]{0:T(1024)S(1)} %copy-done.61), kind=kOutput, calls=%fused_computation.87 | convolution fusion | flops 4305977344 | bytes 31469568 | tf_op jit(solution)/shard_map/dot_general | solution.py:26
  737.5 13.0 %fusion.128 = f32[4096,1024]{1,0:T(8,128)} fusion(bf16[512,4096]{1,0:T(8,128)(2,1)} %get-tuple-element.417, f32[]{:T(128)} %bitcast.28, bf16[2,512,1024]{2,1,0:T(8,128)(2,1)} %param.27), kind=kOutput, calls=%fused_computation.214 | convolution fusion | flops 4296540160 | bytes 22020608 | tf_op jit(solution)/shard_map/dot_general | solution.py:26
  750.4 11.5 %add_convert_fusion = bf16[4096,1024]{1,0:T(8,128)(2,1)} fusion(f32[4096,1024]{1,0:T(8,128)} %fusion.128, bf16[512,4096]{1,0:T(8,128)(2,1)} %get-tuple-element.418, f32[]{:T(128)} %bitcast.41, bf16[2,512,1024]{2,1,0:T(8,128)(2,1)S(1)} %copy-done.39), kind=kOutput, calls=%fused_computation.86 | convolution fusion | flops 4304928768 | bytes 30408708 | tf_op jit(solution)/shard_map/dot_general | solution.py:26
  784.9 58.0 %all-reduce.17 = (bf16[1024]{0:T(1024)(128)(2,1)S(1)}, bf16[1024]{0:T(1024)(128)(2,1)S(1)}, bf16[1024]{0:T(1024)(128)(2,1)S(1)}, bf16[1024]{0:T(1024)(128)(2,1)S...) all-reduce(bf16[1024]{0:T(1024)(128)(2,1)S(1)} %dynamic-update-slic, ...), channel_id=1, replica_groups=mesh['fsdp'=16,'seq'=2] {'fsdp'}, use_global_device_ids=true, to_apply=%add.7 | all-reduce | flops 13312 | bytes 53248
  872.3 48.5 %reduce-scatter.15.cloned.1.call-done = bf16[64,4096]{1,0:T(8,128)(2,1)} async-done(((bf16[1024,4096]{1,0:T(8,128)(2,1)}), bf16[64,4096]{1,0:T(8,128)(2,1)}) %reduce-scatter.15.cloned.1.call-update) | async-done | bytes 524304 | tf_op jit(solution)/shard_map/reduce_scatter | solution.py:189
  920.8 107.0 %reduce-scatter.17.cloned.1.call-done = bf16[256,1024]{1,0:T(8,128)(2,1)} async-done(((bf16[4096,1024]{1,0:T(8,128)(2,1)}), bf16[256,1024]{1,0:T(8,128)(2,1)}) %reduce-scatter.17.cloned.1.call-update) | async-done | bytes 524304 | tf_op jit(solution)/shard_map/reduce_scatter | solution.py:195
  1036.4 45.3 %all-reduce.23.cloned.1.call-done = (bf16[64,1024]{1,0:T(8,128)(2,1)}, bf16[64,1024]{1,0:T(8,128)(2,1)}, bf16[64,1024]{1,0:T(8,128)(2,1)}, bf16[64,1024]{1,0:T(8...) async-done(((bf16[64,1024]{1,0:T(8,128)(2,1)}, bf16[64,1024]{1,0:T(8,128)(2,1)}, bf16[64,1024]{1,0:T(8,128)(2,1)}, bf16[64,1024]{1,0:T(8,128)(2,1)}, ...) | async-done | bytes 1572880 | tf_op jit(solution)/shard_map/psum | solution.py:205
  (466 shorter events, 544.7 us)
Async XLA Ops:
  7.2 77.3 %all-gather.12.cloned.1.call-start = ((), (), s32[]{:S(2)}) async-start(), calls=%async_computation.24 | async-start | bytes 2228224 | tf_op jit(solution)/shard_map/all_gather | solution.py:140
  7.9 89.1 %all-gather.8.cloned.1.call-start = ((), (), s32[]{:S(2)}) async-start(), calls=%async_computation.22 | async-start | bytes 2228224 | tf_op jit(solution)/shard_map/all_gather | solution.py:138
  8.7 130.8 %all-gather.10.cloned.1.call-start = ((), (), s32[]{:S(2)}) async-start(), calls=%async_computation.23 | async-start | bytes 2228224 | tf_op jit(solution)/shard_map/all_gather | solution.py:139
  9.4 274.6 %all-gather.14.cloned.1.call-start = ((), (), s32[]{:S(2)}) async-start(), calls=%async_computation.25 | async-start | bytes 2228224 | tf_op jit(solution)/shard_map/all_gather | solution.py:143
  10.0 293.4 %all-gather.16.cloned.1.call-start = ((), (), s32[]{:S(2)}) async-start(), calls=%async_computation.26 | async-start | bytes 8912896 | tf_op jit(solution)/shard_map/all_gather | solution.py:147
  101.8 41.7 %all-to-all-start = ((bf16[512,2,512]{2,0,1:T(8,128)(2,1)}), bf16[512,2,512]{2,0,1:T(8,128)(2,1)}, u32[]{:S(2)}, u32[]{:S(2)}) async-start(bf16[512,2,512]{2,0,1:T(8,128)(2,1)} %bitcast.451), calls=%async_computation | async-start | bytes 2097152 | tf_op jit(solution)/shard_map/all_to_all | solution.py:254
  143.4 17.8 %all-to-all-start.1 = ((bf16[512,2,512]{2,0,1:T(8,128)(2,1)}), bf16[512,2,512]{2,0,1:T(8,128)(2,1)S(1)}, u32[]{:S(2)}, u32[]{:S(2)}) async-start(bf16[512,2,512]{2,0,1:T(8,128)(2,1)} %bitcast.450), calls=%async_computation.1 | async-start | bytes 2097152 | tf_op jit(solution)/shard_map/all_to_all | solution.py:255
  162.2 29.9 %all-to-all-start.6 = ((bf16[512,2,512]{2,0,1:T(8,128)(2,1)}), bf16[512,2,512]{2,0,1:T(8,128)(2,1)S(1)}, u32[]{:S(2)}, u32[]{:S(2)}) async-start(bf16[512,2,512]{2,0,1:T(8,128)(2,1)} %bitcast.447), calls=%async_computation.6 | async-start | bytes 2097152 | tf_op jit(solution)/shard_map/all_to_all | solution.py:256
  165.9 165.8 %all-gather.18.cloned.1.call-start = ((), (), s32[]{:S(2)}) async-start(), calls=%async_computation.27 | async-start | bytes 8912896 | tf_op jit(solution)/shard_map/all_gather | solution.py:149
  192.1 20.5 %all-to-all-start.5 = ((bf16[512,2,512]{2,0,1:T(8,128)(2,1)}), bf16[512,2,512]{2,0,1:T(8,128)(2,1)}, u32[]{:S(2)}, u32[]{:S(2)}) async-start(bf16[512,2,512]{2,0,1:T(8,128)(2,1)} %bitcast.448), calls=%async_computation.5 | async-start | bytes 2097152 | tf_op jit(solution)/shard_map/all_to_all | solution.py:255
  212.6 37.3 %all-to-all-start.4 = ((bf16[512,2,512]{2,0,1:T(8,128)(2,1)}), bf16[512,2,512]{2,0,1:T(8,128)(2,1)}, u32[]{:S(2)}, u32[]{:S(2)}) async-start(bf16[512,2,512]{2,0,1:T(8,128)(2,1)} %bitcast.446), calls=%async_computation.4 | async-start | bytes 2097152 | tf_op jit(solution)/shard_map/all_to_all | solution.py:254
  249.8 29.5 %all-to-all-start.3 = ((bf16[2,512,512]{1,2,0:T(8,128)(2,1)}), bf16[2,512,512]{1,2,0:T(8,128)(2,1)}, u32[]{:S(2)}, u32[]{:S(2)}) async-start(bf16[2,512,512]{1,2,0:T(8,128)(2,1)} %bitcast.14), calls=%async_computation.3 | async-start | bytes 2097152 | tf_op jit(solution)/shard_map/all_to_all | solution.py:259
  279.3 19.4 %all-to-all-start.7 = ((bf16[2,512,512]{1,2,0:T(8,128)(2,1)}), bf16[2,512,512]{1,2,0:T(8,128)(2,1)}, u32[]{:S(2)}, u32[]{:S(2)}) async-start(bf16[2,512,512]{1,2,0:T(8,128)(2,1)} %bitcast.24), calls=%async_computation.7 | async-start | bytes 2097152 | tf_op jit(solution)/shard_map/all_to_all | solution.py:259
  384.3 17.8 %all-to-all-start.8 = ((bf16[512,2,512]{2,0,1:T(8,128)(2,1)}), bf16[512,2,512]{2,0,1:T(8,128)(2,1)S(1)}, u32[]{:S(2)}, u32[]{:S(2)}) async-start(bf16[512,2,512]{2,0,1:T(8,128)(2,1)} %bitcast.449), calls=%async_computation.8 | async-start | bytes 2097152 | tf_op jit(solution)/shard_map/all_to_all | solution.py:284
  387.9 484.4 %reduce-scatter.13.cloned.1.call-start = ((), (), s32[]{:S(2)}) async-start(), calls=%async_computation.31 | async-start | bytes 2228224 | tf_op jit(solution)/shard_map/reduce_scatter | solution.py:177
  403.2 100.5 %all-to-all-start.12 = ((bf16[512,2,512]{2,0,1:T(8,128)(2,1)}), bf16[512,2,512]{2,0,1:T(8,128)(2,1)}, u32[]{:S(2)}, u32[]{:S(2)}) async-start(bf16[512,2,512]{2,0,1:T(8,128)(2,1)} %bitcast.355), calls=%async_computation.12 | async-start | bytes 2097152 | tf_op jit(solution)/shard_map/all_to_all | solution.py:284
  503.6 99.7 %all-to-all-start.11 = ((bf16[2,512,512]{1,2,0:T(8,128)(2,1)}), bf16[2,512,512]{1,2,0:T(8,128)(2,1)}, u32[]{:S(2)}, u32[]{:S(2)}) async-start(bf16[2,512,512]{1,2,0:T(8,128)(2,1)} %copy.129), calls=%async_computation.11 | async-start | bytes 2097152 | tf_op jit(solution)/shard_map/all_to_all | solution.py:291
  607.0 265.3 %reduce-scatter.11.cloned.1.call-start = ((), (), s32[]{:S(2)}) async-start(), calls=%async_computation.30 | async-start | bytes 2228224 | tf_op jit(solution)/shard_map/reduce_scatter | solution.py:168
  633.4 17.1 %all-to-all-start.10 = ((bf16[2,512,512]{1,2,0:T(8,128)(2,1)}), bf16[2,512,512]{1,2,0:T(8,128)(2,1)}, u32[]{:S(2)}, u32[]{:S(2)}) async-start(bf16[2,512,512]{1,2,0:T(8,128)(2,1)} %copy.128), calls=%async_computation.10 | async-start | bytes 2097152 | tf_op jit(solution)/shard_map/all_to_all | solution.py:290
  654.9 217.4 %reduce-scatter.9.cloned.1.call-start = ((), (), s32[]{:S(2)}) async-start(), calls=%async_computation.29 | async-start | bytes 2228224 | tf_op jit(solution)/shard_map/reduce_scatter | solution.py:165
  691.9 180.4 %reduce-scatter.7.cloned.1.call-start = ((), (), s32[]{:S(2)}) async-start(), calls=%async_computation.28 | async-start | bytes 2228224 | tf_op jit(solution)/shard_map/reduce_scatter | solution.py:162
  707.6 213.2 %reduce-scatter.15.cloned.1.call-start = ((), (), s32[]{:S(2)}) async-start(), calls=%async_computation.32 | async-start | bytes 8912896 | tf_op jit(solution)/shard_map/reduce_scatter | solution.py:189
  737.4 290.4 %reduce-scatter.17.cloned.1.call-start = ((), (), s32[]{:S(2)}) async-start(), calls=%async_computation.33 | async-start | bytes 8912896 | tf_op jit(solution)/shard_map/reduce_scatter | solution.py:195
  762.1 319.7 %all-reduce.23.cloned.1.call-start = ((), (), s32[]{:S(2)}) async-start(), calls=%async_computation.34 | async-start | bytes 3145728 | tf_op jit(solution)/shard_map/psum | solution.py:205
  (104 other events, 1536.2 us)
Sparse Core Ops, SparseCore 0:
  10.2 44.2 all-gather.11
  56.6 40.3 all-gather.7
  99.2 40.1 all-gather.9
  141.4 40.1 all-gather.13
  183.7 73.0 all-gather.15
  258.7 72.8 all-gather.17
  393.2 60.8 reduce-scatter.12
  625.6 59.6 reduce-scatter.10
  689.0 60.7 reduce-scatter.8
  753.4 60.8 reduce-scatter.6
  818.4 102.4 reduce-scatter.14
  924.7 103.0 reduce-scatter.16
  1030.5 51.2 all-reduce.22
where the time goes:
time: 1110 us; the launch traced here: 1100 us
  matrix products  381 us (34%)
  waiting for transfers between devices  301 us (27%)
  blocking collectives  161 us (15%)
  other arithmetic  95 us (9%)
  local copies, waits for them, and re-layouts  73.8 us (7%)
  starting transfers between devices  64.7 us (6%)
  between operations  18.8 us (2%)
    unnamed x2, blocking collectives  121 us
    reduce_scatter x1, waiting for transfers between devices, settle(): lax.psum_scatter(grads[13].astype(jnp.bfloat16), 'fsdp', scatter_dimensio...  107 us
    dot_general x12, matrix products, matmul_tn(): lax.dot_general(left, right, (((0,), (0,)), ((), ())), preferred_element_...  94.3 us
    dot_general x12, matrix products, matmul(): return jnp.dot(left, right, preferred_element_type=jnp.float32)  62.4 us
    dot_general x12, matrix products, matmul_nt(): lax.dot_general(left, right, (((1,), (1,)), ((), ())), preferred_element_...  62.1 us
    reduce_scatter x1, waiting for transfers between devices, settle(): lax.psum_scatter(grads[11].astype(jnp.bfloat16), 'fsdp', scatter_dimensio...  48.5 us
    psum x1, waiting for transfers between devices, settle(): lax.psum(shares[2].astype(jnp.bfloat16), 'seq').astype(jnp.float32)  45.3 us
    dot_general x4, matrix products, one_block(): jnp.einsum('qhd,khd->hqk', grad_rows, value_heads, preferred_element_type...  43.2 us
  transfers between devices with their start and end apart: 28, of which 14 were waited for; matrix products, arithmetic and copies ran while one was open for 44% of the time, Pallas kernels for 0%

commit v1 on v0

--- a/solution.py
+++ b/solution.py
@@ -1,6 +1,8 @@
 import jax
 import jax.numpy as jnp
 from jax import lax
+from jax.experimental import pallas as pl
+from jax.experimental.pallas import tpu as pltpu
 from jax.sharding import PartitionSpec as P
 
 H = 16
@@ -400,6 +402,375 @@
     )
 
 
+T, D, FF, NTILE = 1024, 1024, 4096, 8
+
+log2_e = 1.4426950408889634
+HD = 64
+F32, BF16 = jnp.float32, jnp.bfloat16
+ANY = pl.BlockSpec(memory_space=pl.ANY)
+
+
+def dot(left, right, cl=1, cr=0):
+    return lax.dot_general(left, right, (((cl,), (cr,)), ((), ())), preferred_element_type=F32)
+
+
+def fwd_compute(x_v, sm_v, wqkv, wp_v, w1_v, w2_v, n1t, qkvt, ot, lse_v, mid, n2, acc, hst, gst, b1_v, smt,
+                get_tile, put_tile, hooks):
+    T, D = x_v.shape
+    tile = hst.shape[2]
+    FF = w1_v.shape[1]
+    heads = D // HD
+    smt[...] = jnp.transpose(sm_v[...])
+
+    def ln1(i, c):
+        r = pl.multiple_of(i * 256, 256)
+        v = x_v[pl.ds(r, 256), :].astype(F32)
+        m = jnp.mean(v, axis=-1, keepdims=True)
+        d = v - m
+        s = d * lax.rsqrt(jnp.mean(d * d, axis=-1, keepdims=True) + norm_eps)
+        n1t[:, pl.ds(r, 256)] = jnp.transpose((s * sm_v[0:1, :] + sm_v[1:2, :]).astype(BF16))
+        return c
+
+    lax.fori_loop(0, T // 256, ln1, 0)
+    hooks.before_qkv()
+    half = D // 2
+    for j in range(3):
+        for o in range(2):
+            v = dot(wqkv[j, :, o * half:(o + 1) * half], n1t[...], 0, 0)
+            if j != 1:
+                v = v + smt[o * half:(o + 1) * half, (2 if j == 0 else 3):(3 if j == 0 else 4)]
+            qkvt[j, o * half:(o + 1) * half, :] = v.astype(BF16)
+        hooks.qkv_tick(j)
+
+    qb = T // 2
+    ones = jnp.ones((16, T), BF16)
+
+    def head(h, c):
+        r = pl.multiple_of(h * HD, HD)
+        kh = qkvt[1, pl.ds(r, HD), :]
+        vh = jnp.concatenate([qkvt[2, pl.ds(r, HD), :], ones], axis=0)
+        for b in range(2):
+            qh = qkvt[0, pl.ds(r, HD), b * qb:(b + 1) * qb]
+            s = dot(kh, qh, 0, 0)
+            m = jnp.max(s, axis=0, keepdims=True)
+            p = jnp.exp2((s - m) * (log2_e * HD ** -0.5)).astype(BF16)
+            o = dot(vh, p)
+            total = o[HD:HD + 1, :]
+            ot[pl.ds(r, HD), b * qb:(b + 1) * qb] = (o[:HD, :] / total).astype(BF16)
+            lse_v[pl.ds(h, 1), b * qb:(b + 1) * qb] = m * HD ** -0.5 + jnp.log(total)
+        return c
+
+    def pair(i, c):
+        head(2 * i, c)
+        head(2 * i + 1, c)
+        hooks.attn_tick(i)
+        return c
+
+    lax.fori_loop(0, heads // 2, pair, 0)
+    hooks.before_proj()
+
+    def proj(i, c):
+        r = pl.multiple_of(i * 512, 512)
+        v = dot(ot[:, pl.ds(r, 512)], wp_v[...], 0, 0) + x_v[pl.ds(r, 512), :].astype(F32) + sm_v[4:5, :]
+        mid[pl.ds(r, 512), :] = v
+        m = jnp.mean(v, axis=-1, keepdims=True)
+        d = v - m
+        s = d * lax.rsqrt(jnp.mean(d * d, axis=-1, keepdims=True) + norm_eps)
+        n2[pl.ds(r, 512), :] = (s * sm_v[5:6, :] + sm_v[6:7, :]).astype(BF16)
+        acc[pl.ds(r, 512), :] = v + sm_v[7:8, :]
+        return c
+
+    lax.fori_loop(0, T // 512, proj, 0)
+    for k in range(FF // tile):
+        kk = k * tile
+        b1_v[k:k + 1, :] = sm_v[8 + kk // D:9 + kk // D, kk % D:kk % D + tile]
+    hooks.before_mlp()
+
+    def mlp(j, c):
+        t = get_tile(j)
+        slot = j % 2
+        col = pl.multiple_of(t * tile, tile)
+        hooks.mlp_tick(j)
+
+        def rows(i, c2):
+            r = pl.multiple_of(i * 512, 512)
+            u = dot(n2[pl.ds(r, 512), :], w1_v[:, pl.ds(col, tile)]) + b1_v[pl.ds(t, 1), :]
+            cdf = 0.5 + 0.5 * lax.erf(u * root_half)
+            hb = (u * cdf).astype(BF16)
+            hst[slot, pl.ds(r, 512), :] = hb
+            gst[slot, pl.ds(r, 512), :] = (cdf + (u * inv_root_tau) * jnp.exp2(u * u * (-0.5 * log2_e))).astype(BF16)
+            acc[pl.ds(r, 512), :] += dot(hb, w2_v[pl.ds(col, tile), :])
+            return c2
+
+        lax.fori_loop(0, T // 512, rows, 0)
+        put_tile(j, t, slot)
+        return c
+
+    lax.fori_loop(0, FF // tile, mlp, 0)
+
+
+class NoHooks:
+    def __getattr__(self, name):
+        return lambda *a: None
+
+
+def split3(v):
+    hi = v.astype(BF16)
+    r = v - hi.astype(F32)
+    md = r.astype(BF16)
+    lo = (r - md.astype(F32)).astype(BF16)
+    return hi, md, lo
+
+
+def aug_rows(v):
+    hi, md, lo = split3(v)
+    z = jnp.zeros((13, v.shape[1]), BF16)
+    return jnp.concatenate([hi, md, lo, z], axis=0)
+
+
+def bwd_mlp(g, n2, gacc, h, gp, w1t, w2t, sg_v, j, t, col_slot, put_w2, put_w1):
+    gb = g[...]
+    put_w2(dot(h[col_slot], gb, 0, 0).astype(BF16))
+    pre = (dot(gb, w2t[col_slot], 1, 1) * gp[col_slot].astype(F32)).astype(BF16)
+    gp[col_slot] = pre
+    sg_v[pl.ds(t, 1), :] = jnp.sum(pre.astype(F32), axis=0, keepdims=True)
+    put_w1(dot(n2[...], pre, 0, 0).astype(BF16))
+    v = dot(pre, w1t[col_slot], 1, 1)
+
+    @pl.when(j == 0)
+    def _():
+        gacc[...] = v
+
+    @pl.when(j > 0)
+    def _():
+        gacc[...] += v
+
+
+def ln_back(up, v, gain):
+    m = jnp.mean(v, axis=-1, keepdims=True)
+    d = v - m
+    r = lax.rsqrt(jnp.mean(d * d, axis=-1, keepdims=True) + norm_eps)
+    xh = d * r
+    s = up * gain
+    back = r * (s - jnp.mean(s, axis=-1, keepdims=True) - xh * jnp.mean(s * xh, axis=-1, keepdims=True))
+    return back, jnp.sum(up * xh, axis=0, keepdims=True), jnp.sum(up, axis=0, keepdims=True)
+
+
+def bwd_head(h, qkvt, ot, dot_v, lse_v):
+    T = ot.shape[1]
+    qb = T // 2
+    scale = HD ** -0.5
+    r = pl.multiple_of(h * HD, HD)
+    rows = pl.ds(r, HD)
+    ones = jnp.ones((16, T), BF16)
+    kh = qkvt[1, rows, :]
+    ka = jnp.concatenate([kh, ones], axis=0)
+    va = jnp.concatenate([qkvt[2, rows, :], ones], axis=0)
+    dk = dv = None
+    for b in range(2):
+        cols = slice(b * qb, (b + 1) * qb)
+        qh = qkvt[0, rows, cols] * jnp.asarray(scale, BF16)
+        do = dot_v[rows, cols]
+        delta = jnp.sum(do.astype(F32) * ot[rows, cols].astype(F32), axis=0, keepdims=True)
+        qa = jnp.concatenate([qh, aug_rows(-lse_v[pl.ds(h, 1), cols])], axis=0)
+        da = jnp.concatenate([do, aug_rows(-delta)], axis=0)
+        p = jnp.exp2(dot(qa, ka, 0, 0) * log2_e)
+        ds = (p * dot(da, va, 0, 0)).astype(BF16)
+        ndv = dot(do, p.astype(BF16))
+        ndk = dot(qh, ds)
+        dv = ndv if dv is None else dv + ndv
+        dk = ndk if dk is None else dk + ndk
+        qkvt[0, rows, cols] = (dot(kh, ds, 1, 1) * scale).astype(BF16)
+    qkvt[1, rows, :] = dk.astype(BF16)
+    qkvt[2, rows, :] = dv.astype(BF16)
+
+
+def fwd_kernel(x,sm,wqkv,wp,w1,w2, out,n1t_o,qkvt_o,ot_o,lse_o,mid_o,n2_o,h_o,g_o, x_v,sm_v,wqkv_v,wp_v,w1_v,w2_v,n1t,qkvt,ot,lse_v,mid,n2,acc,hst,gst,b1_v,smt,sem,osem,tsem):
+    ins=[(x,x_v),(sm,sm_v),(wqkv,wqkv_v),(wp,wp_v),(w1,w1_v),(w2,w2_v)]
+    cps=[pltpu.make_async_copy(a,b,sem.at[i]) for i,(a,b) in enumerate(ins)]
+    for c in cps: c.start()
+    for c in cps: c.wait()
+    tile=hst.shape[2]
+    def tcp(j,t,slot,k):
+        return pltpu.make_async_copy((hst,gst)[k].at[slot],(h_o,g_o)[k].at[t],tsem.at[slot,k])
+    class Hk(NoHooks):
+        def mlp_tick(self,j):
+            @pl.when(j>=2)
+            def _():
+                for k in range(2): tcp(j-2,j-2,j%2,k).wait()
+    def put(j,t,slot):
+        for k in range(2): tcp(j,t,slot,k).start()
+    fwd_compute(x_v,sm_v,wqkv_v,wp_v,w1_v,w2_v,n1t,qkvt,ot,lse_v,mid,n2,acc,hst,gst,b1_v,smt,lambda j:j,put,Hk())
+    for j in (6,7):
+        for k in range(2): tcp(j,j,j%2,k).wait()
+    x_v[...]=acc[...].astype(BF16)
+    outs=[(x_v,out),(n1t,n1t_o),(qkvt,qkvt_o),(ot,ot_o),(lse_v,lse_o),(mid,mid_o),(n2,n2_o)]
+    cps=[pltpu.make_async_copy(a,b,osem.at[i]) for i,(a,b) in enumerate(outs)]
+    for c in cps: c.start()
+    for c in cps: c.wait()
+
+
+def bwd_kernel(cot,x,sm,wqkv,wp,w1,w2,n1t,qkvt,ot,lse,mid,n2,hs,gs, gx,dqkv,dwp,dw1,dw2,sg,
+  g_v,n2_v,gacc,h_v,gp_v,w1_v,w2_v,b1g,mid_v,qkvt_v,ot_v,do_v,lse_v,n1t_v,x_v,sm_v,sg_v,st_v,gx_v,sem,tsem,osem,msem,xsem):
+    def cp(a,b,i):
+        return pltpu.make_async_copy(a,b,sem.at[i])
+    first=[cp(cot,g_v,0),cp(n2,n2_v,1),cp(sm,sm_v,2)]
+    later=[cp(qkvt,qkvt_v,3),cp(ot,ot_v,4),cp(lse,lse_v,5),cp(n1t,n1t_v,6),cp(x,x_v,7)]
+    def tl(t,s):
+        c=pl.multiple_of(t*512,512)
+        return [pltpu.make_async_copy(hs.at[t],h_v.at[s],tsem.at[s,0]),pltpu.make_async_copy(gs.at[t],gp_v.at[s],tsem.at[s,1]),
+          pltpu.make_async_copy(w1.at[:,pl.ds(c,512)],w1_v.at[s],tsem.at[s,2]),pltpu.make_async_copy(w2.at[pl.ds(c,512),:],w2_v.at[s],tsem.at[s,3])]
+    for c in first: c.start()
+    for c in tl(0,0): c.start()
+    for c in later: c.start()
+    for c in first: c.wait()
+    sg_v[...]=jnp.zeros_like(sg_v)
+    sg_v[7:8,:]=jnp.sum(g_v[...].astype(F32),axis=0,keepdims=True)
+    def wcp(k,t):
+        c=pl.multiple_of(t*512,512)
+        return pltpu.make_async_copy(st_v.at[k],dw2.at[pl.ds(c,512),:],osem.at[k]) if k==0 else pltpu.make_async_copy(st_v.at[k].reshape(1024,512) if False else n_st(k),dw1.at[:,pl.ds(c,512)],osem.at[k])
+    def n_st(k): return st1_v
+    st1_v=gx_v
+    def tile(j,c):
+        s=j%2
+        @pl.when(j+1<NTILE)
+        def _():
+            for c_ in tl(j+1,1-s): c_.start()
+        for c_ in tl(j,s): c_.wait()
+        def p2(v):
+            @pl.when(j>0)
+            def _(): wcp(0,j-1).wait()
+            st_v[0]=v; wcp(0,j).start()
+        def p1(v):
+            @pl.when(j>0)
+            def _(): wcp(1,j-1).wait()
+            st1_v[...]=v; wcp(1,j).start()
+        bwd_mlp(g_v,n2_v,gacc,h_v,gp_v,w1_v,w2_v,b1g,j,j,s,p2,p1)
+        return c
+    lax.fori_loop(0,NTILE,tile,0)
+    wcp(0,NTILE-1).wait(); wcp(1,NTILE-1).wait()
+    for k in range(NTILE):
+        kk=k*512
+        sg_v[8+kk//D:9+kk//D,kk%D:kk%D+512]=b1g[k:k+1,:]
+    wpl=[pltpu.make_async_copy(wp.at[i*512:(i+1)*512,:],w2_v.at[i],tsem.at[i,3]) for i in range(2)]
+    for c in wpl: c.start()
+    wl=[]
+    for j in range(3):
+        for i in range(2):
+            wl.append(pltpu.make_async_copy(wqkv.at[j,:,i*512:(i+1)*512],(h_v,gp_v,w1_v)[j].at[i],tsem.at[i,j]))
+    for c in wl: c.start()
+    def ml(i,s): return pltpu.make_async_copy(mid.at[pl.ds(pl.multiple_of(i*256,256),256),:],mid_v.at[s],msem.at[s])
+    ml(0,0).start()
+    def ln2(i,c):
+        r=pl.multiple_of(i*256,256); s=i%2
+        @pl.when(i<3)
+        def _(): ml(i+1,1-s).start()
+        ml(i,s).wait()
+        back,dg,db=ln_back(gacc[pl.ds(r,256),:],mid_v[s],sm_v[5:6,:])
+        gm=g_v[pl.ds(r,256),:].astype(F32)+back
+        gacc[pl.ds(r,256),:]=gm
+        gb=gm.astype(BF16)
+        g_v[pl.ds(r,256),:]=gb
+        sg_v[5:6,:]+=dg; sg_v[6:7,:]+=db; sg_v[4:5,:]+=jnp.sum(gb.astype(F32),axis=0,keepdims=True)
+        return c
+    lax.fori_loop(0,4,ln2,0)
+    for c in later: c.wait()
+    for c in wpl: c.wait()
+    for i in range(2):
+        st_v[i]=dot(ot_v[i*512:(i+1)*512,:],g_v[...]).astype(BF16)
+        do_v[i*512:(i+1)*512,:]=dot(w2_v[i],g_v[...],1,1).astype(BF16)
+    op=[pltpu.make_async_copy(st_v.at[i],dwp.at[i*512:(i+1)*512,:],osem.at[i]) for i in range(2)]
+    for c in op: c.start()
+    def hd(h,c):
+        bwd_head(h,qkvt_v,ot_v,do_v,lse_v)
+        return c
+    lax.fori_loop(0,16,hd,0)
+    for c in op: c.wait()
+    for c in wl: c.wait()
+    ones=jnp.ones((16,T),BF16)
+    for j in (0,2):
+        sg_v[(2,None,3)[j]:(3,None,4)[j],:]=dot(ones,qkvt_v[j],1,1)[0:1,:]
+    def ocp(j,i): return pltpu.make_async_copy(st_v.at[i],dqkv.at[j,i*512:(i+1)*512,:],osem.at[i])
+    for j in range(3):
+        for i in range(2):
+            if j>0: ocp(j-1,i).wait()
+            st_v[i]=dot(n1t_v[i*512:(i+1)*512,:],qkvt_v[j],1,1).astype(BF16)
+            ocp(j,i).start()
+    for i in range(2): ocp(2,i).wait()
+    def xcp(i,s): return pltpu.make_async_copy(mid_v.at[s],gx.at[pl.ds(pl.multiple_of(i*256,256),256),:],xsem.at[s])
+    def fin(i,c):
+        r=pl.multiple_of(i*256,256); s=i%2
+        up=None
+        for j,b in enumerate((h_v,gp_v,w1_v)):
+            for k in range(2):
+                v=dot(qkvt_v[j,k*512:(k+1)*512,pl.ds(r,256)],b[k],0,1)
+                up=v if up is None else up+v
+        back,dg,db=ln_back(up,x_v[pl.ds(r,256),:].astype(F32),sm_v[0:1,:])
+        @pl.when(i>=2)
+        def _(): xcp(i-2,s).wait()
+        mid_v[s]=gacc[pl.ds(r,256),:]+back
+        xcp(i,s).start()
+        sg_v[0:1,:]+=dg; sg_v[1:2,:]+=db
+        return c
+    lax.fori_loop(0,4,fin,0)
+    xcp(2,0).wait(); xcp(3,1).wait()
+    c=pltpu.make_async_copy(sg_v,sg,sem.at[0]); c.start(); c.wait()
+
+
+S = jax.ShapeDtypeStruct
+V = pltpu.VMEM
+
+def fwd_call():
+    return pl.pallas_call(fwd_kernel,name="k1",in_specs=[ANY]*6,out_specs=[ANY]*9,
+     out_shape=[S((T,D),BF16),S((D,T),BF16),S((3,D,T),BF16),S((D,T),BF16),S((16,T),F32),S((T,D),F32),S((T,D),BF16),S((8,T,512),BF16),S((8,T,512),BF16)],
+     scratch_shapes=[pltpu.VMEM((T,D),BF16),pltpu.VMEM((16,D),F32),pltpu.VMEM((3,D,D),BF16),pltpu.VMEM((D,D),BF16),pltpu.VMEM((D,FF),BF16),pltpu.VMEM((FF,D),BF16),
+      pltpu.VMEM((D,T),BF16),pltpu.VMEM((3,D,T),BF16),pltpu.VMEM((D,T),BF16),pltpu.VMEM((16,T),F32),pltpu.VMEM((T,D),F32),pltpu.VMEM((T,D),BF16),pltpu.VMEM((T,D),F32),
+      pltpu.VMEM((2,T,512),BF16),pltpu.VMEM((2,T,512),BF16),pltpu.VMEM((8,512),F32),pltpu.VMEM((D,16),F32),
+      pltpu.SemaphoreType.DMA((8,)),pltpu.SemaphoreType.DMA((8,)),pltpu.SemaphoreType.DMA((2,2))],
+     compiler_params=pltpu.CompilerParams(vmem_limit_bytes=63<<20))
+
+
+def bwd_call():
+    return pl.pallas_call(bwd_kernel,name="k2",in_specs=[ANY]*15,out_specs=[ANY]*6,
+     out_shape=[S((T,D),F32),S((3,D,D),BF16),S((D,D),BF16),S((D,FF),BF16),S((FF,D),BF16),S((16,D),F32)],
+     scratch_shapes=[V((T,D),BF16),V((T,D),BF16),V((T,D),F32),V((2,T,512),BF16),V((2,T,512),BF16),V((2,D,512),BF16),V((2,512,D),BF16),V((8,512),F32),V((2,256,D),F32),
+      V((3,D,T),BF16),V((D,T),BF16),V((D,T),BF16),V((16,T),F32),V((D,T),BF16),V((T,D),BF16),V((16,D),F32),V((16,D),F32),V((2,512,D),BF16),V((D,512),BF16),
+      pltpu.SemaphoreType.DMA((8,)),pltpu.SemaphoreType.DMA((2,4)),pltpu.SemaphoreType.DMA((2,)),pltpu.SemaphoreType.DMA((2,)),pltpu.SemaphoreType.DMA((2,))],
+     compiler_params=pltpu.CompilerParams(vmem_limit_bytes=63<<20))
+
+
+def fast_body(clips, cotangent, valid, *shards):
+    me = lax.axis_index("fsdp")
+    mine = lax.axis_index("seq")
+    x = lax.all_to_all(clips, "seq", split_axis=0, concat_axis=1, tiled=True)[0]
+    flag = valid[mine].astype(jnp.bfloat16)
+    cot = lax.all_to_all(cotangent, "seq", split_axis=0, concat_axis=1, tiled=True)[0] * flag
+    (g1, b1, wq, wk, wv, bq, bv, wp, bp, g2, b2, w1, fb1, w2, fb2) = shards
+    gather = lambda v, axis=0: lax.all_gather(v, "fsdp", axis=axis, tiled=True)
+    packed = gather(jnp.concatenate([g1, b1, bq, bv, bp, g2, b2, fb2, fb1])[None])
+    n = g1.shape[0]
+    vecs = packed[:, : 8 * n].reshape(-1, 8, n).transpose(1, 0, 2).reshape(8, -1)
+    fvec = packed[:, 8 * n :].reshape(-1, D)
+    sm = jnp.concatenate([vecs, fvec, jnp.zeros((4, D), jnp.bfloat16)]).astype(jnp.float32)
+    wqkv = gather(jnp.stack([wq, wk, wv]), 1)
+    wp_all, w1_all, w2_all = gather(wp), gather(w1), gather(w2)
+    out, *saved = fwd_call()(x, sm, wqkv, wp_all, w1_all, w2_all)
+    gx, dqkv, dwp, dw1, dw2, sg = bwd_call()(cot, x, sm, wqkv, wp_all, w1_all, w2_all, *saved)
+    back = lambda v: lax.all_to_all(v[None], "seq", split_axis=1, concat_axis=0, tiled=True)
+
+    def total(v, axis=0):
+        part = lax.psum_scatter(v, "fsdp", scatter_dimension=axis, tiled=True)
+        return lax.psum(part, "seq").astype(jnp.float32)
+
+    dw2, dw1, dqkv, dwp = total(dw2), total(dw1), total(dqkv, 1), total(dwp)
+    sg = lax.psum(sg, ("fsdp", "seq"))
+    own = lax.dynamic_slice(sg[:8], (0, me * n), (8, n))
+    m = fb1.shape[0]
+    dfb1 = lax.dynamic_slice(sg[8:12].reshape(-1), (me * m,), (m,))
+    gx = back(gx.astype(jnp.bfloat16)).astype(jnp.float32)
+    return (back(out), gx, own[0], own[1], dqkv[0], dqkv[1], dqkv[2], own[2], own[3], dwp, own[4], own[5], own[6], dw1, dfb1, dw2, own[7])
+
+
 def solution(mesh):
     in_specs = (
         P("fsdp", "seq", None),
@@ -440,4 +811,5 @@
         P("fsdp", None),
         P("fsdp"),
     )
-    return jax.shard_map(body, mesh=mesh, in_specs=in_specs, out_specs=out_specs, check_vma=False)
+    quick = mesh.shape["seq"] == 2 and mesh.shape["fsdp"] == 16
+    return jax.shard_map(fast_body if quick else body, mesh=mesh, in_specs=in_specs, out_specs=out_specs, check_vma=False)

time: 1110 us -> 1050 us (0.946)
  matrix products: 381 us -> 0 us
  waiting for transfers between devices: 301 us -> 662 us
  Pallas kernels: 0 us -> 219 us
  blocking collectives: 161 us -> 52.2 us
  other arithmetic: 95 us -> 37.5 us
  starting transfers between devices: 64.7 us -> 14.2 us
  local copies, waits for them, and re-layouts: 73.8 us -> 40.8 us
    dot_general x64 -> x0, matrix products: 381 us -> none  [the longest x12 94.3 us: matmul_tn(): lax.dot_general(left, right, (((0,), (0,)), ((), ())), preferred_element_...]
    pallas_call x0 -> x2, Pallas kernels: none -> 219 us  [the longest x1 136 us: fast_body(): bwd_call()(cot, x, sm, wqkv, wp_all, w1_all, w2_all, *saved)]
    reduce_scatter x6 -> x4, waiting for transfers between devices: 156 us -> 332 us  [total(): part = lax.psum_scatter(v, 'fsdp', scatter_dimension=axis, tiled=True)]
    all_gather x6 -> x4, waiting for transfers between devices: 43.9 us -> 195 us  [fast_body(): gather = lambda v, axis=0: lax.all_gather(v, 'fsdp', axis=axis, tiled=True)]
    unnamed x2 -> x0, blocking collectives: 121 us -> none
    psum x1 -> x2, waiting for transfers between devices: 45.3 us -> 131 us  [the longest x1 95.5 us: fast_body(): sg = lax.psum(sg, ('fsdp', 'seq'))]
    convert_element_type x39 -> x5, other arithmetic: 61.8 us -> 4.71 us  [the longest x4 4 us: total(): return lax.psum(part, 'seq').astype(jnp.float32)]
    all_to_all x15 -> x3, waiting for transfers between devices: 52.4 us -> 0.01 us  [the longest x2 0.01 us: fast_body(): lax.all_to_all(v[None], 'seq', split_axis=1, concat_axis=0, tiled=True)]
  transfers between devices with their start and end apart: 28 -> 13, of which waited for: 14 -> 9; matrix products, arithmetic and copies ran while one was open for 44% -> 7% of each run, Pallas kernels for 0% -> 0%
where the time goes in v1:
time: 1050 us; the launch traced here: 1040 us
  waiting for transfers between devices  662 us (63%)
  Pallas kernels  219 us (21%)
  blocking collectives  52.2 us (5%)
  local copies, waits for them, and re-layouts  40.8 us (4%)
  other arithmetic  37.5 us (4%)
  between operations  15.5 us (1%)
  starting transfers between devices  14.2 us (1%)
    reduce_scatter x4, waiting for transfers between devices, total(): part = lax.psum_scatter(v, 'fsdp', scatter_dimension=axis, tiled=True)  332 us
    all_gather x4, waiting for transfers between devices, fast_body(): gather = lambda v, axis=0: lax.all_gather(v, 'fsdp', axis=axis, tiled=True)  195 us
    pallas_call x1, Pallas kernels, fast_body(): bwd_call()(cot, x, sm, wqkv, wp_all, w1_all, w2_all, *saved)  136 us
    psum x1, waiting for transfers between devices, fast_body(): sg = lax.psum(sg, ('fsdp', 'seq'))  95.5 us
    pallas_call x1, Pallas kernels, fast_body(): out, *saved = fwd_call()(x, sm, wqkv, wp_all, w1_all, w2_all)  83.3 us
    psum x1, waiting for transfers between devices, total(): return lax.psum(part, 'seq').astype(jnp.float32)  35.4 us
    all_to_all x1, blocking collectives, fast_body(): lax.all_to_all(cotangent, 'seq', split_axis=0, concat_axis=1, tiled=True)[0]  30.1 us
    unnamed x2, other arithmetic  26.9 us
  transfers between devices with their start and end apart: 13, of which 9 were waited for; matrix products, arithmetic and copies ran while one was open for 7% of the time, Pallas kernels for 0%

profile of v1, /device:TPU:0, one launch (start us, length us, event | category | flops | bytes accessed | tf_op | source)
XLA Modules:
  0.0 1041.7 jit_solution(7984369002854518201)
XLA Ops:
  11.1 30.1 %all_to_all.19 = bf16[2,512,1024]{2,1,0:T(8,128)(2,1)S(1)} all-to-all(bf16[2,512,1024]{2,1,0:T(8,128)(2,1)} %param.19), channel_id=1, replica_groups=mesh['fsdp'=16,'seq'=2] {'seq'}, dimensions={0} | all-to-all | bytes 4194304 | tf_op jit(solution)/shard_map/all_to_all | solution.py:747
  41.3 5.0 all-to-all-start
  46.6 22.1 %all-gather.1 = bf16[16,1,768]{2,1,0:T(2,128)(2,1)S(1)} all-gather(bf16[1,1,768]{2,1,0:T(2,128)(2,1)S(1)} %reshape.71), channel_id=2, replica_groups=mesh['fsdp'=16,'seq'=2] {'fsdp'}, dimensions={0}, use_global_device_ids=true | all-gather | bytes 26112 | tf_op jit(solution)/shard_map/all_gather | solution.py:749
  72.4 44.9 %all-gather.7.cloned.1.call-done.wqkv = bf16[3,1024,1024]{2,1,0:T(8,128)(2,1)} async-done(((bf16[3,64,1024]{2,1,0:T(8,128)(2,1)}), bf16[3,1024,1024]{2,1,0:T(8,128)(2,1)}) %all-gather.7.cloned.1.call-update) | async-done | bytes 6291472 | tf_op jit(solution)/shard_map/all_gather | solution.py:749
  117.3 75.2 %all-gather.11.cloned.1.call-done.w1 = bf16[1024,4096]{1,0:T(8,128)(2,1)} async-done(((bf16[64,4096]{1,0:T(8,128)(2,1)}), bf16[1024,4096]{1,0:T(8,128)(2,1)}) %all-gather.11.cloned.1.call-update) | async-done | bytes 8388624 | tf_op jit(solution)/shard_map/all_gather | solution.py:749
  192.5 74.9 %all-gather.13.cloned.1.call-done.w2 = bf16[4096,1024]{1,0:T(8,128)(2,1)} async-done(((bf16[256,1024]{1,0:T(8,128)(2,1)}), bf16[4096,1024]{1,0:T(8,128)(2,1)}) %all-gather.13.cloned.1.call-update) | async-done | bytes 8388624 | tf_op jit(solution)/shard_map/all_gather | solution.py:749
  267.4 83.3 %k1.1 = (bf16[1024,1024]{1,0:T(8,128)(2,1)}, bf16[1024,1024]{1,0:T(8,128)(2,1)}, bf16[3,1024,1024]{2,1,0:T(8,128)(2,1)}, bf16[1024,1024]{1,0:T(8,128)(2,1)}, f32...) custom-call(bf16[1024,1024]{1,0:T(8,128)(2,1)} %bitcast.x, ...), custom_call_target="tpu_custom_call" | custom-call | tf_op jit(solution)/shard_map/k1/pallas_call | solution.py:757
  350.7 136.2 %k2.1 = (f32[1024,1024]{1,0:T(8,128)}, bf16[3,1024,1024]{2,1,0:T(8,128)(2,1)}, bf16[1024,1024]{1,0:T(8,128)(2,1)}, bf16[1024,4096]{1,0:T(8,128)(2,1)}, bf16[4096,1024]{1,0:T(8,128)(2,1)}, /*index=5*/f32[16,1024]{1,0:T(8,128)}) custom-call(bf16[1024,1024]{1,0:T(8,128)(2,1)} %bitcast.56, bf16[1024,1024]{1,0:T(8,128)(2,1)} %bitcast.x, ...), custom_call_target="tpu_custom_call" | custom-call | tf_op jit(solution)/shard_map/k2/pallas_call | solution.py:758
  491.6 5.2 copy.54
  497.4 12.8 %reduce.1 = bf16[1024,1024]{1,0:T(8,128)(2,1)S(1)} reduce(bf16[1024,1,1024]{2,1,0:T(2,128)(2,1)} %bitcast.52, bf16[]{:T(256)} %broadcast.4), dimensions={1}, to_apply=%bitcast.50.reduce_sub_computation | reduce | bytes 4194306
  512.8 3.8 all-to-all-start.3
  517.5 30.0 %reduce-scatter.7.cloned.1.call-done = bf16[64,1024]{1,0:T(8,128)(2,1)} async-done(((bf16[1024,1024]{1,0:T(8,128)(2,1)}), bf16[64,1024]{1,0:T(8,128)(2,1)}) %reduce-scatter.7.cloned.1.call-update) | async-done | bytes 131088 | tf_op jit(solution)/shard_map/reduce_scatter | solution.py:762
  547.5 87.8 %reduce-scatter.5.cloned.1.call-done = bf16[3,64,1024]{2,1,0:T(8,128)(2,1)} async-done(((bf16[3,1024,1024]{2,1,0:T(8,128)(2,1)}), bf16[3,64,1024]{2,1,0:T(8,128)(2,1)}) %reduce-scatter.5.cloned.1.call-update) | async-done | bytes 393232 | tf_op jit(solution)/shard_map/reduce_scatter | solution.py:762
  635.3 106.7 %reduce-scatter.11.cloned.1.call-done = bf16[256,1024]{1,0:T(8,128)(2,1)} async-done(((bf16[4096,1024]{1,0:T(8,128)(2,1)}), bf16[256,1024]{1,0:T(8,128)(2,1)}) %reduce-scatter.11.cloned.1.call-update) | async-done | bytes 524304 | tf_op jit(solution)/shard_map/reduce_scatter | solution.py:762
  742.0 107.2 %reduce-scatter.9.cloned.1.call-done = bf16[64,4096]{1,0:T(8,128)(2,1)} async-done(((bf16[1024,4096]{1,0:T(8,128)(2,1)}), bf16[64,4096]{1,0:T(8,128)(2,1)}) %reduce-scatter.9.cloned.1.call-update) | async-done | bytes 524304 | tf_op jit(solution)/shard_map/reduce_scatter | solution.py:762
  849.2 6.8 copy.55
  856.0 14.1 %reduce = bf16[1024,1024]{1,0:T(8,128)(2,1)} reduce(bf16[1024,1,1024]{2,1,0:T(2,128)(2,1)} %bitcast.53, bf16[]{:T(256)} %broadcast.4), dimensions={1}, to_apply=%bitcast.51.reduce_sub_computation | reduce | bytes 4194306
  870.1 3.9 reshape.74
  874.0 4.9 all-to-all-start.1
  878.9 95.5 %all-reduce.4.cloned.1.call-done = f32[16,1024]{1,0:T(8,128)} async-done(((f32[16,1024]{1,0:T(8,128)}), f32[16,1024]{1,0:T(8,128)}) %all-reduce.4.cloned.1.call-update) | async-done | bytes 65552 | tf_op jit(solution)/shard_map/psum | solution.py:766
  980.3 5.2 copy.44
  985.5 4.3 reshape.75
  989.8 4.4 copy.43
  994.2 35.4 %all-reduce.6.cloned.1.call-done = (bf16[3,64,1024]{2,1,0:T(8,128)(2,1)}, bf16[64,1024]{1,0:T(8,128)(2,1)}, bf16[64,4096]{1,0:T(8,128)(2,1)}, bf16[256,1024]{1,0:T(8,128)(2,1)}) async-done(((bf16[3,64,1024]{2,1,0:T(8,128)(2,1)}, bf16[64,1024]{1,0:T(8,128)(2,1)}, bf16[64,4096]{1,0:T(8,128)(2,1)}, bf16[256,1024]{1,0:T(8,128)(2,1)}), (bf16[3,64,1024]{2,1,0:T(8,128)(2,1)}, bf16[64,1024]{1,0:T(8,128)(2,1)}, ...) | async-done | bytes 1572880 | tf_op jit(solution)/shard_map/psum | solution.py:763
  (80 shorter events, 26.6 us)
Async XLA Ops:
  7.2 65.2 %all-gather.9.cloned.1.call-start = ((), (), s32[]{:S(2)}) async-start(), calls=%async_computation.9 | async-start | bytes 2228224 | tf_op jit(solution)/shard_map/all_gather | solution.py:749
  7.9 109.4 %all-gather.7.cloned.1.call-start = ((), (), s32[]{:S(2)}) async-start(), calls=%async_computation.8 | async-start | bytes 6684672 | tf_op jit(solution)/shard_map/all_gather | solution.py:749
  9.8 182.7 %all-gather.11.cloned.1.call-start = ((), (), s32[]{:S(2)}) async-start(), calls=%async_computation.10 | async-start | bytes 8912896 | tf_op jit(solution)/shard_map/all_gather | solution.py:749
  10.6 256.9 %all-gather.13.cloned.1.call-start = ((), (), s32[]{:S(2)}) async-start(), calls=%async_computation.11 | async-start | bytes 8912896 | tf_op jit(solution)/shard_map/all_gather | solution.py:749
  41.3 5.1 copy-start.3
  41.3 5.1 copy-start.4
  41.3 5.1 copy-start.5
  41.3 5.1 copy-start.6
  41.3 5.2 copy-start.7
  41.3 5.2 copy-start.8
  41.3 5.1 copy-start.9
  41.3 5.1 copy-start.10
  41.3 5.1 copy-start.11
  41.3 27.5 %copy-start.12 = (s32[2]{0:T(128)S(1)}, s32[2]{0:T(128)}, u32[]{:S(2)}) copy-start(s32[2]{0:T(128)} %param.20) | copy-start | bytes 28
  41.3 31.0 %all-to-all-start = ((bf16[2,512,1024]{2,1,0:T(8,128)(2,1)}), bf16[2,512,1024]{2,1,0:T(8,128)(2,1)}, u32[]{:S(2)}, u32[]{:S(2)}) async-start(bf16[2,512,1024]{2,1,0:T(8,128)(2,1)} %param.18), calls=%async_computation | async-start | bytes 4194304 | tf_op jit(solution)/shard_map/all_to_all | solution.py:745
  46.3 501.2 %reduce-scatter.7.cloned.1.call-start = ((), (), s32[]{:S(2)}) async-start(), calls=%async_computation.14 | async-start | bytes 2228224 | tf_op jit(solution)/shard_map/reduce_scatter | solution.py:762
  487.0 148.4 %reduce-scatter.5.cloned.1.call-start = ((), (), s32[]{:S(2)}) async-start(), calls=%async_computation.13 | async-start | bytes 6684672 | tf_op jit(solution)/shard_map/reduce_scatter | solution.py:762
  487.5 254.4 %reduce-scatter.11.cloned.1.call-start = ((), (), s32[]{:S(2)}) async-start(), calls=%async_computation.16 | async-start | bytes 8912896 | tf_op jit(solution)/shard_map/reduce_scatter | solution.py:762
  488.3 360.9 %reduce-scatter.9.cloned.1.call-start = ((), (), s32[]{:S(2)}) async-start(), calls=%async_computation.15 | async-start | bytes 8912896 | tf_op jit(solution)/shard_map/reduce_scatter | solution.py:762
  512.8 361.2 %all-to-all-start.3 = ((bf16[2,2,262144]{2,1,0:T(2,128)(2,1)}), bf16[2,2,262144]{2,1,0:T(2,128)(2,1)S(1)}, u32[]{:S(2)}, u32[]{:S(2)}) async-start(bf16[2,2,262144]{2,1,0:T(2,128)(2,1)} %reshape.76), calls=%async_computation.3 | async-start | bytes 4194304 | tf_op jit(solution)/shard_map/all_to_all | solution.py:759
  516.5 457.9 %all-reduce.4.cloned.1.call-start = ((), (), s32[]{:S(2)}) async-start(), calls=%async_computation.12 | async-start | bytes 131072 | tf_op jit(solution)/shard_map/psum | solution.py:766
  517.3 512.3 %all-reduce.6.cloned.1.call-start = ((), (), s32[]{:S(2)}) async-start(), calls=%async_computation.17 | async-start | bytes 3145728 | tf_op jit(solution)/shard_map/psum | solution.py:763
  874.0 111.5 %all-to-all-start.1 = ((bf16[2,2,262144]{2,1,0:T(2,128)(2,1)}), bf16[2,2,262144]{2,1,0:T(2,128)(2,1)}, u32[]{:S(2)}, u32[]{:S(2)}) async-start(bf16[2,2,262144]{2,1,0:T(2,128)(2,1)} %reshape.74), calls=%async_computation.1 | async-start | bytes 4194304 | tf_op jit(solution)/shard_map/all_to_all | solution.py:759
  1029.6 3.1 copy-start
  (2 other events, 5.1 us)
Sparse Core Ops, SparseCore 0:
  10.2 44.1 all-gather.8
  57.1 60.1 all-gather.6
  119.5 72.9 all-gather.10
  194.5 72.8 all-gather.12
  487.1 60.3 reduce-scatter.6
  551.3 83.9 reduce-scatter.4
  639.4 102.5 reduce-scatter.10
  746.0 103.0 reduce-scatter.8
  855.3 119.0 all-reduce.3
  976.7 52.8 all-reduce.5

commit v2 on v1

--- a/solution.py
+++ b/solution.py
@@ -1,3 +1,4 @@
+import functools
 import jax
 import jax.numpy as jnp
 from jax import lax
@@ -414,106 +415,6 @@
     return lax.dot_general(left, right, (((cl,), (cr,)), ((), ())), preferred_element_type=F32)
 
 
-def fwd_compute(x_v, sm_v, wqkv, wp_v, w1_v, w2_v, n1t, qkvt, ot, lse_v, mid, n2, acc, hst, gst, b1_v, smt,
-                get_tile, put_tile, hooks):
-    T, D = x_v.shape
-    tile = hst.shape[2]
-    FF = w1_v.shape[1]
-    heads = D // HD
-    smt[...] = jnp.transpose(sm_v[...])
-
-    def ln1(i, c):
-        r = pl.multiple_of(i * 256, 256)
-        v = x_v[pl.ds(r, 256), :].astype(F32)
-        m = jnp.mean(v, axis=-1, keepdims=True)
-        d = v - m
-        s = d * lax.rsqrt(jnp.mean(d * d, axis=-1, keepdims=True) + norm_eps)
-        n1t[:, pl.ds(r, 256)] = jnp.transpose((s * sm_v[0:1, :] + sm_v[1:2, :]).astype(BF16))
-        return c
-
-    lax.fori_loop(0, T // 256, ln1, 0)
-    hooks.before_qkv()
-    half = D // 2
-    for j in range(3):
-        for o in range(2):
-            v = dot(wqkv[j, :, o * half:(o + 1) * half], n1t[...], 0, 0)
-            if j != 1:
-                v = v + smt[o * half:(o + 1) * half, (2 if j == 0 else 3):(3 if j == 0 else 4)]
-            qkvt[j, o * half:(o + 1) * half, :] = v.astype(BF16)
-        hooks.qkv_tick(j)
-
-    qb = T // 2
-    ones = jnp.ones((16, T), BF16)
-
-    def head(h, c):
-        r = pl.multiple_of(h * HD, HD)
-        kh = qkvt[1, pl.ds(r, HD), :]
-        vh = jnp.concatenate([qkvt[2, pl.ds(r, HD), :], ones], axis=0)
-        for b in range(2):
-            qh = qkvt[0, pl.ds(r, HD), b * qb:(b + 1) * qb]
-            s = dot(kh, qh, 0, 0)
-            m = jnp.max(s, axis=0, keepdims=True)
-            p = jnp.exp2((s - m) * (log2_e * HD ** -0.5)).astype(BF16)
-            o = dot(vh, p)
-            total = o[HD:HD + 1, :]
-            ot[pl.ds(r, HD), b * qb:(b + 1) * qb] = (o[:HD, :] / total).astype(BF16)
-            lse_v[pl.ds(h, 1), b * qb:(b + 1) * qb] = m * HD ** -0.5 + jnp.log(total)
-        return c
-
-    def pair(i, c):
-        head(2 * i, c)
-        head(2 * i + 1, c)
-        hooks.attn_tick(i)
-        return c
-
-    lax.fori_loop(0, heads // 2, pair, 0)
-    hooks.before_proj()
-
-    def proj(i, c):
-        r = pl.multiple_of(i * 512, 512)
-        v = dot(ot[:, pl.ds(r, 512)], wp_v[...], 0, 0) + x_v[pl.ds(r, 512), :].astype(F32) + sm_v[4:5, :]
-        mid[pl.ds(r, 512), :] = v
-        m = jnp.mean(v, axis=-1, keepdims=True)
-        d = v - m
-        s = d * lax.rsqrt(jnp.mean(d * d, axis=-1, keepdims=True) + norm_eps)
-        n2[pl.ds(r, 512), :] = (s * sm_v[5:6, :] + sm_v[6:7, :]).astype(BF16)
-        acc[pl.ds(r, 512), :] = v + sm_v[7:8, :]
-        return c
-
-    lax.fori_loop(0, T // 512, proj, 0)
-    for k in range(FF // tile):
-        kk = k * tile
-        b1_v[k:k + 1, :] = sm_v[8 + kk // D:9 + kk // D, kk % D:kk % D + tile]
-    hooks.before_mlp()
-
-    def mlp(j, c):
-        t = get_tile(j)
-        slot = j % 2
-        col = pl.multiple_of(t * tile, tile)
-        hooks.mlp_tick(j)
-
-        def rows(i, c2):
-            r = pl.multiple_of(i * 512, 512)
-            u = dot(n2[pl.ds(r, 512), :], w1_v[:, pl.ds(col, tile)]) + b1_v[pl.ds(t, 1), :]
-            cdf = 0.5 + 0.5 * lax.erf(u * root_half)
-            hb = (u * cdf).astype(BF16)
-            hst[slot, pl.ds(r, 512), :] = hb
-            gst[slot, pl.ds(r, 512), :] = (cdf + (u * inv_root_tau) * jnp.exp2(u * u * (-0.5 * log2_e))).astype(BF16)
-            acc[pl.ds(r, 512), :] += dot(hb, w2_v[pl.ds(col, tile), :])
-            return c2
-
-        lax.fori_loop(0, T // 512, rows, 0)
-        put_tile(j, t, slot)
-        return c
-
-    lax.fori_loop(0, FF // tile, mlp, 0)
-
-
-class NoHooks:
-    def __getattr__(self, name):
-        return lambda *a: None
-
-
 def split3(v):
     hi = v.astype(BF16)
     r = v - hi.astype(F32)
@@ -585,29 +486,336 @@
     qkvt[2, rows, :] = dv.astype(BF16)
 
 
-def fwd_kernel(x,sm,wqkv,wp,w1,w2, out,n1t_o,qkvt_o,ot_o,lse_o,mid_o,n2_o,h_o,g_o, x_v,sm_v,wqkv_v,wp_v,w1_v,w2_v,n1t,qkvt,ot,lse_v,mid,n2,acc,hst,gst,b1_v,smt,sem,osem,tsem):
-    ins=[(x,x_v),(sm,sm_v),(wqkv,wqkv_v),(wp,wp_v),(w1,w1_v),(w2,w2_v)]
-    cps=[pltpu.make_async_copy(a,b,sem.at[i]) for i,(a,b) in enumerate(ins)]
-    for c in cps: c.start()
-    for c in cps: c.wait()
-    tile=hst.shape[2]
-    def tcp(j,t,slot,k):
-        return pltpu.make_async_copy((hst,gst)[k].at[slot],(h_o,g_o)[k].at[t],tsem.at[slot,k])
-    class Hk(NoHooks):
-        def mlp_tick(self,j):
-            @pl.when(j>=2)
-            def _():
-                for k in range(2): tcp(j-2,j-2,j%2,k).wait()
-    def put(j,t,slot):
-        for k in range(2): tcp(j,t,slot,k).start()
-    fwd_compute(x_v,sm_v,wqkv_v,wp_v,w1_v,w2_v,n1t,qkvt,ot,lse_v,mid,n2,acc,hst,gst,b1_v,smt,lambda j:j,put,Hk())
-    for j in (6,7):
-        for k in range(2): tcp(j,j,j%2,k).wait()
-    x_v[...]=acc[...].astype(BF16)
-    outs=[(x_v,out),(n1t,n1t_o),(qkvt,qkvt_o),(ot,ot_o),(lse_v,lse_o),(mid,mid_o),(n2,n2_o)]
-    cps=[pltpu.make_async_copy(a,b,osem.at[i]) for i,(a,b) in enumerate(outs)]
-    for c in cps: c.start()
-    for c in cps: c.wait()
+MESH = pl.DeviceIdType.MESH
+
+
+class Place:
+    def __init__(self, size):
+        f = lax.axis_index("fsdp")
+        self.f, self.core, chip = f, f % 2, f // 2
+        self.deep, self.count = size // 4, size // 2
+        x, z = chip % 2, chip // 2
+        self.pos = z + x * (2 * self.deep - 1 - 2 * z)
+        self.mate = f + 1 - 2 * self.core
+        self.y = lax.axis_index("seq")
+
+    def chip(self, off):
+        pos = (self.pos + self.count + off) % self.count
+        hi = pos // self.deep
+        return 2 * (pos + hi * (2 * self.deep - 1 - 2 * pos)) + hi
+
+    def side(self, d):
+        return {"fsdp": 2 * self.chip((1, -1)[d]) + self.core}
+
+    def partner(self):
+        return {"fsdp": self.mate}
+
+    def across(self):
+        return {"seq": 1 - self.y}
+
+    def barrier(self):
+        sem = pltpu.get_barrier_semaphore()
+        for dev in (self.side(0), self.side(1), self.partner(), self.across()):
+            pl.semaphore_signal(sem, inc=1, device_id=dev, device_id_type=MESH)
+        pl.semaphore_wait(sem, 4)
+
+
+def remote(src, dst, ss, rs, dev):
+    return pltpu.make_async_remote_copy(src_ref=src, dst_ref=dst, send_sem=ss, recv_sem=rs, device_id=dev, device_id_type=MESH)
+
+
+class Gather:
+    def __init__(self, place, view, rsem, psem):
+        self.pl, self.view, self.rsem, self.psem = place, view, rsem, psem
+        self.last = place.count // 2 - 1
+
+    def part(self, d, s):
+        return d if s == self.last else 2
+
+    def block(self, d, s, ahead):
+        k = s + ahead
+        return self.pl.chip(-k if d == 0 else k)
+
+    def ring(self, d, s, ahead=0):
+        v = self.view(2 * self.block(d, s, ahead) + self.pl.core, self.part(d, s))
+        return remote(v, v, self.rsem.at[0, d, s], self.rsem.at[1, d, s], self.pl.side(d))
+
+    def mate(self, slot, chip, part, core):
+        v = self.view(2 * chip + core, part)
+        return remote(v, v, self.psem.at[0, slot], self.psem.at[1, slot], self.pl.partner())
+
+    def slots(self, s):
+        return [(1 + 2 * s + d, self.block(d, s, 1), self.part(d, s)) for d in range(2)]
+
+    def start(self):
+        for d in range(2):
+            self.ring(d, 0).start()
+        self.mate(0, self.pl.chip(0), 2, self.pl.core).start()
+
+    def step(self, s):
+        for d in range(2):
+            self.ring(d, s, 1).wait_recv()
+            if s < self.last:
+                self.ring(d, s + 1).start()
+        for slot, chip, part in self.slots(s):
+            self.mate(slot, chip, part, self.pl.core).start()
+
+    def own_mate(self):
+        self.mate(0, self.pl.chip(0), 2, 1 - self.pl.core).wait_recv()
+
+    def step_mate(self, s):
+        for slot, chip, part in self.slots(s):
+            self.mate(slot, chip, part, 1 - self.pl.core).wait_recv()
+
+    def all_mates(self):
+        self.own_mate()
+        for s in range(self.last + 1):
+            self.step_mate(s)
+
+    def drain(self):
+        for s in range(self.last + 1):
+            for d in range(2):
+                self.ring(d, s).wait_send()
+            for slot, chip, part in self.slots(s):
+                self.mate(slot, chip, part, self.pl.core).wait_send()
+        self.mate(0, self.pl.chip(0), 2, self.pl.core).wait_send()
+
+
+def fwd_body(size, clips, cot, sml, wq, wk, wv, wp, w1, w2,
+             out_o, cot_o, x_o, sm_o, wqkv_o, wp_o, w1_o, w2_o, n1t_o, qkvt_o, ot_o, lse_o, mid_o, n2_o, h_o, g_o,
+             x_v, smb, sm_v, wqkv_v, wp_v, w1_v, w2_v, n1t, qkvt, ot, lse_v, mid, n2, acc, hst, gst, b1_v, smt,
+             rsem, psem, xsem, lsem, osem, tsem):
+    here = Place(size)
+    T, D = x_v.shape
+    FF = w1_v.shape[1]
+    tile = hst.shape[2]
+    heads = D // HD
+    half = T // 2
+    nd, nf = D // size, FF // size
+    y = here.y
+    ymine = pl.ds(pl.multiple_of(y * half, half), half)
+    yother = pl.ds(pl.multiple_of((1 - y) * half, half), half)
+
+    def local(a, b, i):
+        return pltpu.make_async_copy(a, b, lsem.at[i])
+
+    def rows(ref, n, lead):
+        def view(f, part):
+            k = n if part == 2 else n // 2
+            at = pl.ds(pl.multiple_of(f * n + (n // 2 if part == 1 else 0), k), k)
+            return ref.at[:, at, :] if lead else ref.at[at, :]
+        return view
+
+    def smview(f, part):
+        if part == 2:
+            return smb.at[f]
+        return smb.at[f, :, part * (D // 2):(part + 1) * (D // 2)]
+
+    views = [smview, rows(wqkv_v, nd, True), rows(wp_v, nd, False), rows(w1_v, nd, False), rows(w2_v, nf, False)]
+    ga, gq, gp, g1, g2 = [Gather(here, v, rsem.at[i], psem.at[i]) for i, v in enumerate(views)]
+    own = pl.ds(pl.multiple_of(here.f * nd, nd), nd)
+    ownf = pl.ds(pl.multiple_of(here.f * nf, nf), nf)
+    loc = [local(sml, smb.at[here.f], 0)]
+    loc += [local(w, wqkv_v.at[j, own, :], 1 + j) for j, w in enumerate((wq, wk, wv))]
+    loc += [local(wp, wp_v.at[own, :], 4), local(w1, w1_v.at[own, :], 5), local(w2, w2_v.at[ownf, :], 6), local(clips.at[y], x_v.at[ymine, :], 7)]
+    for c in loc:
+        c.start()
+    here.barrier()
+    xsend = remote(clips.at[1 - y], x_v.at[ymine, :], xsem.at[0, 0], xsem.at[0, 1], here.across())
+    xrecv = remote(clips.at[1 - y], x_v.at[yother, :], xsem.at[0, 0], xsem.at[0, 1], here.across())
+    csend = remote(cot.at[1 - y], cot_o, xsem.at[1, 0], xsem.at[1, 1], here.across())
+    xsend.start()
+    csend.start()
+    for c in loc[:4]:
+        c.wait()
+    ga.start()
+    gq.start()
+    for c in loc[4:]:
+        c.wait()
+
+    def ln1(i, c):
+        r = pl.multiple_of(i * 256, 256)
+        v = x_v[pl.ds(r, 256), :].astype(F32)
+        m = jnp.mean(v, axis=-1, keepdims=True)
+        d = v - m
+        mid[pl.ds(r, 256), :] = d * lax.rsqrt(jnp.mean(d * d, axis=-1, keepdims=True) + norm_eps)
+        return c
+
+    per = half // 256
+    lax.fori_loop(y * per, y * per + per, ln1, 0)
+    for s in range(ga.last + 1):
+        ga.step(s)
+        gq.step(s)
+        if s == ga.last - 1:
+            gp.start()
+            g1.start()
+    xrecv.wait_recv()
+    lax.fori_loop((1 - y) * per, (1 - y) * per + per, ln1, 0)
+    ga.all_mates()
+    sm_v[...] = jnp.sum(smb[...].astype(F32), axis=0)
+    smt[...] = jnp.transpose(sm_v[...])
+
+    def ln1b(i, c):
+        r = pl.multiple_of(i * 256, 256)
+        n1t[:, pl.ds(r, 256)] = jnp.transpose((mid[pl.ds(r, 256), :] * sm_v[0:1, :] + sm_v[1:2, :]).astype(BF16))
+        return c
+
+    lax.fori_loop(0, T // 256, ln1b, 0)
+    gq.all_mates()
+    outs = []
+
+    def save(a, b):
+        c = pltpu.make_async_copy(a, b, osem.at[len(outs)])
+        outs.append(c)
+        c.start()
+
+    save(wqkv_v, wqkv_o)
+    save(x_v, x_o)
+    save(sm_v, sm_o)
+    save(n1t, n1t_o)
+    hd = D // 2
+    for j in range(3):
+        for o in range(2):
+            v = dot(wqkv_v[j, :, o * hd:(o + 1) * hd], n1t[...], 0, 0)
+            if j != 1:
+                v = v + smt[o * hd:(o + 1) * hd, (2 if j == 0 else 3):(3 if j == 0 else 4)]
+            qkvt[j, o * hd:(o + 1) * hd, :] = v.astype(BF16)
+    save(qkvt, qkvt_o)
+    qb = T // 2
+    ones = jnp.ones((16, T), BF16)
+
+    def head(h, c):
+        r = pl.multiple_of(h * HD, HD)
+        kh = qkvt[1, pl.ds(r, HD), :]
+        vh = jnp.concatenate([qkvt[2, pl.ds(r, HD), :], ones], axis=0)
+        for b in range(2):
+            qh = qkvt[0, pl.ds(r, HD), b * qb:(b + 1) * qb]
+            s = dot(kh, qh, 0, 0)
+            m = jnp.max(s, axis=0, keepdims=True)
+            p = jnp.exp2((s - m) * (log2_e * HD ** -0.5)).astype(BF16)
+            o = dot(vh, p)
+            total = o[HD:HD + 1, :]
+            ot[pl.ds(r, HD), b * qb:(b + 1) * qb] = (o[:HD, :] / total).astype(BF16)
+            lse_v[pl.ds(h, 1), b * qb:(b + 1) * qb] = m * HD ** -0.5 + jnp.log(total)
+        return c
+
+    cuts = (0, 3 * heads // 16, 10 * heads // 16, heads)
+    for s in range(3):
+        lax.fori_loop(cuts[s], cuts[s + 1], head, 0)
+        gp.step(s)
+        g1.step(s)
+        if s == 1:
+            g2.start()
+    save(ot, ot_o)
+    save(lse_v, lse_o)
+    for s in range(3, gp.last + 1):
+        gp.step(s)
+    gp.all_mates()
+    save(wp_v, wp_o)
+
+    def proj(i, c):
+        r = pl.multiple_of(i * 512, 512)
+        v = dot(ot[:, pl.ds(r, 512)], wp_v[...], 0, 0) + x_v[pl.ds(r, 512), :].astype(F32) + sm_v[4:5, :]
+        mid[pl.ds(r, 512), :] = v
+        m = jnp.mean(v, axis=-1, keepdims=True)
+        d = v - m
+        s = d * lax.rsqrt(jnp.mean(d * d, axis=-1, keepdims=True) + norm_eps)
+        n2[pl.ds(r, 512), :] = (s * sm_v[5:6, :] + sm_v[6:7, :]).astype(BF16)
+        acc[pl.ds(r, 512), :] = v + sm_v[7:8, :]
+        return c
+
+    lax.fori_loop(0, T // 512, proj, 0)
+    save(mid, mid_o)
+    save(n2, n2_o)
+    for k in range(FF // tile):
+        kk = k * tile
+        b1_v[k:k + 1, :] = sm_v[8 + kk // D:9 + kk // D, kk % D:kk % D + tile]
+    for s in range(3, g1.last + 1):
+        g1.step(s)
+    g2.step(0)
+    g1.all_mates()
+    g2.own_mate()
+    g2.step_mate(0)
+    save(w1_v, w1_o)
+    saves = {}
+    order = [0]
+    for k in range(1, here.count // 2):
+        order += [-k, k]
+    order.append(here.count // 2)
+
+    def tcp(k, slot, t):
+        return pltpu.make_async_copy((hst, gst)[k].at[slot], (h_o, g_o)[k].at[t], tsem.at[k, slot])
+
+    def wcp(j, t):
+        at = pl.ds(pl.multiple_of(t * tile, tile), tile)
+        return pltpu.make_async_copy(w2_v.at[at, :], w2_o.at[at, :], tsem.at[2, j])
+
+    for j, off in enumerate(order):
+        t = here.chip(off)
+        slot = j % 2
+        if j >= 3 and j % 2 == 1:
+            g2.step(j // 2)
+            g2.step_mate(j // 2)
+        wcp(j, t).start()
+        if j >= 2:
+            for k in range(2):
+                tcp(k, slot, here.chip(order[j - 2])).wait()
+        col = pl.multiple_of(t * tile, tile)
+
+        def mlp(i, c, t=t, slot=slot, col=col):
+            r = pl.multiple_of(i * 512, 512)
+            u = dot(n2[pl.ds(r, 512), :], w1_v[:, pl.ds(col, tile)]) + b1_v[pl.ds(t, 1), :]
+            cdf = 0.5 + 0.5 * lax.erf(u * root_half)
+            hb = (u * cdf).astype(BF16)
+            hst[slot, pl.ds(r, 512), :] = hb
+            gst[slot, pl.ds(r, 512), :] = (cdf + (u * inv_root_tau) * jnp.exp2(u * u * (-0.5 * log2_e))).astype(BF16)
+            acc[pl.ds(r, 512), :] += dot(hb, w2_v[pl.ds(col, tile), :])
+            return c
+
+        lax.fori_loop(0, T // 512, mlp, 0)
+        for k in range(2):
+            tcp(k, slot, t).start()
+    for j in range(len(order) - 2, len(order)):
+        for k in range(2):
+            tcp(k, j % 2, here.chip(order[j])).wait()
+    outs[3].wait()
+    n1t[...] = acc[...].astype(BF16)
+    save(n1t, out_o)
+    for j, off in enumerate(order):
+        wcp(j, here.chip(off)).wait()
+    for i, c in enumerate(outs):
+        if i != 3:
+            c.wait()
+    for g in (ga, gq, gp, g1, g2):
+        g.drain()
+    xsend.wait_send()
+    csend.wait_send()
+    remote(cot.at[1 - y], cot_o, xsem.at[1, 0], xsem.at[1, 1], here.across()).wait_recv()
+
+
+S = jax.ShapeDtypeStruct
+V = pltpu.VMEM
+
+
+def fwd_call(size, T, D, FF):
+    tile = 2 * FF // size
+    heads = D // HD
+    small = (16, D)
+    dma = pltpu.SemaphoreType.DMA
+    steps = size // 4
+    return pl.pallas_call(
+        functools.partial(fwd_body, size),
+        name="forward",
+        in_specs=[ANY] * 9,
+        out_specs=[ANY] * 16,
+        out_shape=[S((T, D), BF16), S((T // 2, D), BF16), S((T, D), BF16), S(small, F32), S((3, D, D), BF16), S((D, D), BF16), S((D, FF), BF16), S((FF, D), BF16),
+                   S((D, T), BF16), S((3, D, T), BF16), S((D, T), BF16), S((heads, T), F32), S((T, D), F32), S((T, D), BF16), S((FF // tile, T, tile), BF16), S((FF // tile, T, tile), BF16)],
+        scratch_shapes=[V((T, D), BF16), V((size,) + small, BF16), V(small, F32), V((3, D, D), BF16), V((D, D), BF16), V((D, FF), BF16), V((FF, D), BF16),
+                        V((D, T), BF16), V((3, D, T), BF16), V((D, T), BF16), V((heads, T), F32), V((T, D), F32), V((T, D), BF16), V((T, D), F32),
+                        V((2, T, tile), BF16), V((2, T, tile), BF16), V((FF // tile, tile), F32), V((D, 16), F32),
+                        dma((5, 2, 2, steps)), dma((5, 2, 2 * steps + 1)), dma((2, 2)), dma((8,)), dma((12,)), dma((3, max(2, FF // tile)))],
+        compiler_params=pltpu.CompilerParams(vmem_limit_bytes=63 << 20, collective_id=0, has_side_effects=True),
+    )
 
 
 def bwd_kernel(cot,x,sm,wqkv,wp,w1,w2,n1t,qkvt,ot,lse,mid,n2,hs,gs, gx,dqkv,dwp,dw1,dw2,sg,
@@ -717,19 +925,6 @@
     c=pltpu.make_async_copy(sg_v,sg,sem.at[0]); c.start(); c.wait()
 
 
-S = jax.ShapeDtypeStruct
-V = pltpu.VMEM
-
-def fwd_call():
-    return pl.pallas_call(fwd_kernel,name="k1",in_specs=[ANY]*6,out_specs=[ANY]*9,
-     out_shape=[S((T,D),BF16),S((D,T),BF16),S((3,D,T),BF16),S((D,T),BF16),S((16,T),F32),S((T,D),F32),S((T,D),BF16),S((8,T,512),BF16),S((8,T,512),BF16)],
-     scratch_shapes=[pltpu.VMEM((T,D),BF16),pltpu.VMEM((16,D),F32),pltpu.VMEM((3,D,D),BF16),pltpu.VMEM((D,D),BF16),pltpu.VMEM((D,FF),BF16),pltpu.VMEM((FF,D),BF16),
-      pltpu.VMEM((D,T),BF16),pltpu.VMEM((3,D,T),BF16),pltpu.VMEM((D,T),BF16),pltpu.VMEM((16,T),F32),pltpu.VMEM((T,D),F32),pltpu.VMEM((T,D),BF16),pltpu.VMEM((T,D),F32),
-      pltpu.VMEM((2,T,512),BF16),pltpu.VMEM((2,T,512),BF16),pltpu.VMEM((8,512),F32),pltpu.VMEM((D,16),F32),
-      pltpu.SemaphoreType.DMA((8,)),pltpu.SemaphoreType.DMA((8,)),pltpu.SemaphoreType.DMA((2,2))],
-     compiler_params=pltpu.CompilerParams(vmem_limit_bytes=63<<20))
-
-
 def bwd_call():
     return pl.pallas_call(bwd_kernel,name="k2",in_specs=[ANY]*15,out_specs=[ANY]*6,
      out_shape=[S((T,D),F32),S((3,D,D),BF16),S((D,D),BF16),S((D,FF),BF16),S((FF,D),BF16),S((16,D),F32)],
@@ -740,21 +935,18 @@
 
 
 def fast_body(clips, cotangent, valid, *shards):
+    size = lax.axis_size("fsdp")
     me = lax.axis_index("fsdp")
     mine = lax.axis_index("seq")
-    x = lax.all_to_all(clips, "seq", split_axis=0, concat_axis=1, tiled=True)[0]
-    flag = valid[mine].astype(jnp.bfloat16)
-    cot = lax.all_to_all(cotangent, "seq", split_axis=0, concat_axis=1, tiled=True)[0] * flag
     (g1, b1, wq, wk, wv, bq, bv, wp, bp, g2, b2, w1, fb1, w2, fb2) = shards
-    gather = lambda v, axis=0: lax.all_gather(v, "fsdp", axis=axis, tiled=True)
-    packed = gather(jnp.concatenate([g1, b1, bq, bv, bp, g2, b2, fb2, fb1])[None])
-    n = g1.shape[0]
-    vecs = packed[:, : 8 * n].reshape(-1, 8, n).transpose(1, 0, 2).reshape(8, -1)
-    fvec = packed[:, 8 * n :].reshape(-1, D)
-    sm = jnp.concatenate([vecs, fvec, jnp.zeros((4, D), jnp.bfloat16)]).astype(jnp.float32)
-    wqkv = gather(jnp.stack([wq, wk, wv]), 1)
-    wp_all, w1_all, w2_all = gather(wp), gather(w1), gather(w2)
-    out, *saved = fwd_call()(x, sm, wqkv, wp_all, w1_all, w2_all)
+    n, m = g1.shape[0], fb1.shape[0]
+    vecs = jnp.stack([g1, b1, bq, bv, bp, g2, b2, fb2])
+    sml = lax.dynamic_update_slice(jnp.zeros((8, D), vecs.dtype), vecs, (0, me * n))
+    fsm = lax.dynamic_update_slice(jnp.zeros((FF,), vecs.dtype), fb1, (me * m,)).reshape(-1, D)
+    sml = jnp.concatenate([sml, fsm, jnp.zeros((8 - FF // D, D), vecs.dtype)])
+    out, cot_in, x, sm, wqkv, wp_all, w1_all, w2_all, *saved = fwd_call(size, T, D, FF)(clips, cotangent, sml, wq, wk, wv, wp, w1, w2)
+    both = jnp.concatenate([cotangent[mine], cot_in])
+    cot = jnp.where(mine == 0, both, jnp.roll(both, T // 2, axis=0)) * valid[mine].astype(jnp.bfloat16)
     gx, dqkv, dwp, dw1, dw2, sg = bwd_call()(cot, x, sm, wqkv, wp_all, w1_all, w2_all, *saved)
     back = lambda v: lax.all_to_all(v[None], "seq", split_axis=1, concat_axis=0, tiled=True)
 

time: 1050 us -> 758 us (0.72)
  waiting for transfers between devices: 662 us -> 365 us
  Pallas kernels: 219 us -> 275 us
  blocking collectives: 52.2 us -> 0 us
    all_gather x4 -> x0, waiting for transfers between devices: 195 us -> none  [fast_body(): gather = lambda v, axis=0: lax.all_gather(v, 'fsdp', axis=axis, tiled=True)]
    psum x1, waiting for transfers between devices: 95.5 us -> 0.03 us  [fast_body(): sg = lax.psum(sg, ('fsdp', 'seq'))]
    pallas_call x1, Pallas kernels: 83.3 us -> 149 us  [fast_body(): fwd_call(size, T, D, FF)(clips, cotangent, sml, wq, wk, wv, wp, w1, w2)]
    psum x1, waiting for transfers between devices: 35.4 us -> 0.01 us  [total(): return lax.psum(part, 'seq').astype(jnp.float32)]
    all_to_all x2, waiting for transfers between devices: 0.01 us -> 30.5 us  [fast_body(): lax.all_to_all(v[None], 'seq', split_axis=1, concat_axis=0, tiled=True)]
    all_to_all x1 -> x0, blocking collectives: 30.1 us -> none  [fast_body(): lax.all_to_all(cotangent, 'seq', split_axis=0, concat_axis=1, tiled=True)[0]]
    all_gather x1 -> x0, blocking collectives: 22.1 us -> none  [fast_body(): gather = lambda v, axis=0: lax.all_gather(v, 'fsdp', axis=axis, tiled=True)]
    pallas_call x1, Pallas kernels: 136 us -> 125 us  [fast_body(): bwd_call()(cot, x, sm, wqkv, wp_all, w1_all, w2_all, *saved)]
  transfers between devices with their start and end apart: 13 -> 8, of which waited for: 9 -> 5; matrix products, arithmetic and copies ran while one was open for 7% -> 9% of each run, Pallas kernels for 0% -> 0%
where the time goes in v2:
time: 758 us; the launch traced here: 749 us
  waiting for transfers between devices  365 us (48%)
  Pallas kernels  275 us (36%)
  local copies, waits for them, and re-layouts  43.7 us (6%)
  other arithmetic  38.8 us (5%)
  between operations  16.6 us (2%)
  starting transfers between devices  9.28 us (1%)
    reduce_scatter x4, waiting for transfers between devices, total(): part = lax.psum_scatter(v, 'fsdp', scatter_dimension=axis, tiled=True)  333 us
    pallas_call x1, Pallas kernels, fast_body(): fwd_call(size, T, D, FF)(clips, cotangent, sml, wq, wk, wv, wp, w1, w2)  149 us
    pallas_call x1, Pallas kernels, fast_body(): bwd_call()(cot, x, sm, wqkv, wp_all, w1_all, w2_all, *saved)  125 us
    all_to_all x2, waiting for transfers between devices, fast_body(): lax.all_to_all(v[None], 'seq', split_axis=1, concat_axis=0, tiled=True)  30.5 us
    unnamed x2, other arithmetic  26.9 us
    unnamed x33, local copies, waits for them, and re-layouts  24.7 us
  transfers between devices with their start and end apart: 8, of which 5 were waited for; matrix products, arithmetic and copies ran while one was open for 9% of the time, Pallas kernels for 0%

profile of v2, /device:TPU:0, one launch (start us, length us, event | category | flops | bytes accessed | tf_op | source)
XLA Modules:
  0.0 748.5 jit_solution(12409064258493419007)
XLA Ops:
  9.1 2.3 dynamic-slice_bitcast_fusion
  13.6 149.4 %forward.1 = (bf16[1024,1024]{1,0:T(8,128)(2,1)}, bf16[512,1024]{1,0:T(8,128)(2,1)}, bf16[1024,1024]{1,0:T(8,128)(2,1)}, f32[16,1024]{1,0:T(8,128)}, bf16[3,1024...) custom-call(bf16[2,512,1024]{2,1,0:T(8,128)(2,1)} %clips.1, ...), custom_call_target="tpu_custom_call" | custom-call | tf_op jit(solution)/shard_map/forward/pallas_call | solution.py:947
  163.0 4.7 fusion.cot
  167.7 125.4 %k2.1 = (f32[1024,1024]{1,0:T(8,128)}, bf16[3,1024,1024]{2,1,0:T(8,128)(2,1)}, bf16[1024,1024]{1,0:T(8,128)(2,1)}, bf16[1024,4096]{1,0:T(8,128)(2,1)}, bf16[4096,1024]{1,0:T(8,128)(2,1)}, /*index=5*/f32[16,1024]{1,0:T(8,128)}) custom-call(bf16[1024,1024]{1,0:T(8,128)(2,1)} %fusion.cot, bf16[1024,1024]{1,0:T(8,128)(2,1)} %get-tuple-element.41.x, ...), custom_call_target="tpu_custom_call" | custom-call | tf_op jit(solution)/shard_map/k2/pallas_call | solution.py:950
  295.2 2.5 convert_bitcast_fusion
  297.7 5.2 copy.46
  303.5 12.8 %reduce.1 = bf16[1024,1024]{1,0:T(8,128)(2,1)S(1)} reduce(bf16[1024,1,1024]{2,1,0:T(2,128)(2,1)} %bitcast.51, bf16[]{:T(256)} %broadcast.2), dimensions={1}, to_apply=%bitcast.49.reduce_sub_computation | reduce | bytes 4194306
  316.3 2.6 reshape.54
  318.9 3.8 all-to-all-start.1
  323.5 30.8 %reduce-scatter.7.cloned.1.call-done = bf16[64,1024]{1,0:T(8,128)(2,1)} async-done(((bf16[1024,1024]{1,0:T(8,128)(2,1)}), bf16[64,1024]{1,0:T(8,128)(2,1)}) %reduce-scatter.7.cloned.1.call-update) | async-done | bytes 131088 | tf_op jit(solution)/shard_map/reduce_scatter | solution.py:954
  354.3 88.0 %reduce-scatter.5.cloned.1.call-done = bf16[3,64,1024]{2,1,0:T(8,128)(2,1)} async-done(((bf16[3,1024,1024]{2,1,0:T(8,128)(2,1)}), bf16[3,64,1024]{2,1,0:T(8,128)(2,1)}) %reduce-scatter.5.cloned.1.call-update) | async-done | bytes 393232 | tf_op jit(solution)/shard_map/reduce_scatter | solution.py:954
  442.4 106.7 %reduce-scatter.11.cloned.1.call-done = bf16[256,1024]{1,0:T(8,128)(2,1)} async-done(((bf16[4096,1024]{1,0:T(8,128)(2,1)}), bf16[256,1024]{1,0:T(8,128)(2,1)}) %reduce-scatter.11.cloned.1.call-update) | async-done | bytes 524304 | tf_op jit(solution)/shard_map/reduce_scatter | solution.py:954
  549.0 107.0 %reduce-scatter.9.cloned.1.call-done = bf16[64,4096]{1,0:T(8,128)(2,1)} async-done(((bf16[1024,4096]{1,0:T(8,128)(2,1)}), bf16[64,4096]{1,0:T(8,128)(2,1)}) %reduce-scatter.9.cloned.1.call-update) | async-done | bytes 524304 | tf_op jit(solution)/shard_map/reduce_scatter | solution.py:954
  656.1 6.8 copy.47
  662.9 14.1 %reduce = bf16[1024,1024]{1,0:T(8,128)(2,1)} reduce(bf16[1024,1,1024]{2,1,0:T(2,128)(2,1)} %bitcast.52, bf16[]{:T(256)} %broadcast.2), dimensions={1}, to_apply=%bitcast.50.reduce_sub_computation | reduce | bytes 4194306
  677.0 3.9 reshape.52
  680.9 4.8 all-to-all-start
  688.5 3.1 reshape.55
  691.6 5.2 copy.40
  696.8 30.5 %all-to-all-done = bf16[2,2,262144]{2,1,0:T(2,128)(2,1)} async-done(((bf16[2,2,262144]{2,1,0:T(2,128)(2,1)}), bf16[2,2,262144]{2,1,0:T(2,128)(2,1)}, u32[]{:S(2)}, u32[]{:S(2)}) %all-to-all-start) | async-done | bytes 2097184 | tf_op jit(solution)/shard_map/all_to_all | solution.py:951
  727.4 4.3 reshape.53
  731.7 4.3 copy.39
  736.0 1.2 convert_element_type.32
  739.1 1.1 convert_element_type.35
  (59 shorter events, 11.4 us)
Async XLA Ops:
  8.0 3.3 copy-start.11
  8.0 4.6 copy-start.3
  8.0 4.6 copy-start.4
  8.1 4.6 copy-start.5
  8.1 4.6 copy-start.6
  8.1 4.6 copy-start.7
  8.1 4.6 copy-start.8
  8.1 4.6 copy-start.9
  8.1 4.6 copy-start.10
  8.1 346.2 %reduce-scatter.7.cloned.1.call-start = ((), (), s32[]{:S(2)}) async-start(), calls=%async_computation.8 | async-start | bytes 2228224 | tf_op jit(solution)/shard_map/reduce_scatter | solution.py:954
  293.1 149.2 %reduce-scatter.5.cloned.1.call-start = ((), (), s32[]{:S(2)}) async-start(), calls=%async_computation.7 | async-start | bytes 6684672 | tf_op jit(solution)/shard_map/reduce_scatter | solution.py:954
  293.9 255.1 %reduce-scatter.11.cloned.1.call-start = ((), (), s32[]{:S(2)}) async-start(), calls=%async_computation.10 | async-start | bytes 8912896 | tf_op jit(solution)/shard_map/reduce_scatter | solution.py:954
  294.6 361.4 %reduce-scatter.9.cloned.1.call-start = ((), (), s32[]{:S(2)}) async-start(), calls=%async_computation.9 | async-start | bytes 8912896 | tf_op jit(solution)/shard_map/reduce_scatter | solution.py:954
  318.9 362.0 %all-to-all-start.1 = ((bf16[2,2,262144]{2,1,0:T(2,128)(2,1)}), bf16[2,2,262144]{2,1,0:T(2,128)(2,1)S(1)}, u32[]{:S(2)}, u32[]{:S(2)}) async-start(bf16[2,2,262144]{2,1,0:T(2,128)(2,1)} %reshape.54), calls=%async_computation.1 | async-start | bytes 4194304 | tf_op jit(solution)/shard_map/all_to_all | solution.py:951
  322.6 363.1 %all-reduce.4.cloned.1.call-start = ((), (), s32[]{:S(2)}) async-start(), calls=%async_computation.6 | async-start | bytes 131072 | tf_op jit(solution)/shard_map/psum | solution.py:958
  323.2 412.8 %all-reduce.6.cloned.1.call-start = ((), (), s32[]{:S(2)}) async-start(), calls=%async_computation.11 | async-start | bytes 3145728 | tf_op jit(solution)/shard_map/psum | solution.py:955
  680.9 46.5 %all-to-all-start = ((bf16[2,2,262144]{2,1,0:T(2,128)(2,1)}), bf16[2,2,262144]{2,1,0:T(2,128)(2,1)}, u32[]{:S(2)}, u32[]{:S(2)}) async-start(bf16[2,2,262144]{2,1,0:T(2,128)(2,1)} %reshape.52), calls=%async_computation | async-start | bytes 4194304 | tf_op jit(solution)/shard_map/all_to_all | solution.py:951
  736.0 2.1 copy-start.1
  736.0 3.1 copy-start
  737.2 3.0 copy-start.2
Sparse Core Ops, SparseCore 0:
  293.3 61.0 reduce-scatter.6
  358.3 84.0 reduce-scatter.4
  446.4 102.5 reduce-scatter.10
  552.9 103.0 reduce-scatter.8
Sparse Core Ops, SparseCore 1:
  329.3 136.6 all-reduce.3
  656.1 68.0 all-reduce.5
